TPU v7x, 32 devices: a whole 2x2x4 slice. The times are simulated.
32 devices in a mesh: stn: 16 (over z, y, core), tm: 2 (over x).
Axes of the slice: x: 2, y: 2, z: 4, core: 2. Of those that a mesh axis runs over, the one named last changes fastest.
Arguments:
- voltages: int32 [512, 2, 32768], P('stn', None, 'tm'), may hold values from -127 to 127
- filter_taps: float32 [16, 1024], replicated, may hold values from -1.5 to 1.5
- reference_channel: int32 [1], replicated, may hold values from 0 to 511
- basis_inputs: int32 [8], replicated, may hold values from 0 to 511, as said below
Outputs:
- covariance: bfloat16 [512, 512, 1024], P(('stn', 'tm'))
- projection: float32 [512, 128], P(('stn', 'tm'))
- subspace_power: float32 [512, 32], P('stn', 'tm')
Inputs may be any that keep to these rules, and one draw needn't show every extreme that they name: `basis_inputs`: 8 distinct input indices.
All inputs are finite; a program needn't handle non-finite values.
Results may differ from a plain program's by a relative error of at most 0.012.
Values may be sent and summed in bfloat16 or wider, within the bound.
No kernel may reach another device: no remote copies, remote signals or barrier semaphores. Data moves between devices by JAX's collectives and lax.ppermute only.
A program may use at most 192 MiB of HBM per device.

v0:
```python
import math

import jax
import jax.numpy as jnp
from jax import lax
from jax.sharding import PartitionSpec as P

NFFT = 1024
FCH = 512


def passed_along(block, axis, distance):
    devices = range(lax.axis_size(axis))
    route = [(i - distance, i) for i in devices if i - distance in devices]
    return lax.ppermute(block, axis, route)


def spread(shard, axis, root):
    mine = lax.axis_index(axis) == root
    return lax.psum(jnp.where(mine, shard, jnp.zeros_like(shard)), axis)


def transform_tables():
    sample = jnp.arange(NFFT, dtype=jnp.int32)
    channel = jnp.arange(FCH, dtype=jnp.int32)
    phase = sample[:, None] * channel[None, :] % NFFT
    angle = phase.astype(jnp.float32) * (2.0 * math.pi / NFFT)
    factor = 1.0 / math.sqrt(NFFT)
    cosine = jnp.cos(angle) * factor
    sine = jnp.sin(angle) * factor
    table_re = jnp.stack([cosine, -sine], axis=2).reshape(NFFT, 2 * FCH).astype(jnp.bfloat16)
    table_im = jnp.stack([sine, cosine], axis=2).reshape(NFFT, 2 * FCH).astype(jnp.bfloat16)
    return (table_re, table_im)


def orthonormal(col_real, col_imag):
    basis_real = []
    basis_imag = []
    for column in range(col_real.shape[1]):
        vec_real = col_real[:, column]
        vec_imag = col_imag[:, column]
        for former in range(column):
            q_real = basis_real[former]
            q_imag = basis_imag[former]
            inner_real = jnp.sum(q_real * vec_real + q_imag * vec_imag)
            inner_imag = jnp.sum(q_real * vec_imag - q_imag * vec_real)
            vec_real = vec_real - (q_real * inner_real - q_imag * inner_imag)
            vec_imag = vec_imag - (q_real * inner_imag + q_imag * inner_real)
        inverse = lax.rsqrt(jnp.sum(vec_real * vec_real + vec_imag * vec_imag) + 1e-06)
        basis_real.append(vec_real * inverse)
        basis_imag.append(vec_imag * inverse)
    return (jnp.stack(basis_real, axis=1), jnp.stack(basis_imag, axis=1))


def block_sums(part_real, part_imag):
    sum_real = jnp.einsum("itc,jtc->cij", part_real, part_real, preferred_element_type=jnp.float32)
    sum_real = sum_real + jnp.einsum(
        "itc,jtc->cij", part_imag, part_imag, preferred_element_type=jnp.float32
    )
    sum_imag = jnp.einsum("itc,jtc->cij", part_imag, part_real, preferred_element_type=jnp.float32)
    sum_imag = sum_imag - jnp.einsum(
        "itc,jtc->cij", part_real, part_imag, preferred_element_type=jnp.float32
    )
    return (sum_real, sum_imag)


def blockwise_covariance(full_real, full_imag, blocks, frames):
    inputs_all = full_real.shape[0]
    chans = full_real.shape[2]

    def add_block(index, total):
        first = index * frames
        part_real = lax.dynamic_slice_in_dim(full_real, first, frames, 1)
        part_imag = lax.dynamic_slice_in_dim(full_imag, first, frames, 1)
        sum_real, sum_imag = block_sums(part_real, part_imag)
        terms = jnp.concatenate([sum_real, sum_imag], axis=2)
        rounded = lax.optimization_barrier(terms.astype(jnp.bfloat16)).astype(jnp.float32)
        return total + rounded

    start = jnp.zeros((chans, inputs_all, 2 * inputs_all), jnp.float32)
    return lax.fori_loop(0, blocks, add_block, start)


def on_device(voltages, filter_taps, reference_channel, basis_inputs):
    blocks = lax.axis_size("tm")
    local_inputs = voltages.shape[0]
    inputs_all = local_inputs * lax.axis_size("stn")
    frames = voltages.shape[2] // NFFT
    spectra_total = frames * blocks
    tap_count = filter_taps.shape[0]
    signal = (
        (voltages.astype(jnp.float32) / 64.0)
        .astype(jnp.bfloat16)
        .reshape(local_inputs, 2, frames, NFFT)
    )
    earlier = passed_along(signal[:, :, frames - (tap_count - 1) :, :], "tm", 1)
    extended = jnp.concatenate([earlier, signal], axis=2)
    accum = jnp.zeros((local_inputs, 2, frames, NFFT), jnp.float32)
    for tap_index in range(tap_count):
        accum = accum + filter_taps[tap_index] * extended[
            :, :, tap_index : tap_index + frames, :
        ].astype(jnp.float32)
    filtered = accum.astype(jnp.bfloat16)
    table_re, table_im = transform_tables()
    spectra = jnp.einsum(
        "itn,nc->itc", filtered[:, 0], table_re, preferred_element_type=jnp.float32
    )
    spectra = spectra + jnp.einsum(
        "itn,nc->itc", filtered[:, 1], table_im, preferred_element_type=jnp.float32
    )
    spectra = spectra.astype(jnp.bfloat16)
    rows_iota = jnp.arange(inputs_all, dtype=jnp.int32)[:, None]
    moved = lax.all_to_all(
        lax.all_to_all(spectra, "stn", split_axis=2, concat_axis=0, tiled=True),
        "tm",
        split_axis=2,
        concat_axis=1,
        tiled=True,
    )
    chan_owned = moved.shape[2] // 2
    joined = moved.reshape(inputs_all, spectra_total, chan_owned, 2)
    full_real = joined[:, :, :, 0]
    full_imag = joined[:, :, :, 1]
    summed = blockwise_covariance(full_real, full_imag, blocks, frames)
    averaged = summed / spectra_total
    covariance = averaged.astype(jnp.bfloat16)
    highest = lax.Precision.HIGHEST
    selector = rows_iota == basis_inputs[None, :]
    ref_index = reference_channel[0]
    root_index = ref_index // chan_owned
    local_index = ref_index % chan_owned
    ref_rows = lax.dynamic_slice_in_dim(averaged, local_index, 1, 0)[0]
    onehot = selector.astype(jnp.float32)
    picked = jnp.stack(
        [
            jnp.dot(ref_rows[:, :inputs_all], onehot, precision=highest),
            jnp.dot(ref_rows[:, inputs_all:], onehot, precision=highest),
        ]
    )
    picked = spread(picked.astype(jnp.bfloat16), ("stn", "tm"), root_index).astype(picked.dtype)
    col_real = picked[0]
    col_imag = picked[1]
    basis_real, basis_imag = orthonormal(col_real, col_imag)
    cov_real = averaged[:, :, :inputs_all]
    cov_imag = averaged[:, :, inputs_all:]
    prod_real = jnp.einsum("cij,jk->cik", cov_real, basis_real, precision=highest)
    prod_real = prod_real - jnp.einsum("cij,jk->cik", cov_imag, basis_imag, precision=highest)
    prod_imag = jnp.einsum("cij,jk->cik", cov_real, basis_imag, precision=highest)
    prod_imag = prod_imag + jnp.einsum("cij,jk->cik", cov_imag, basis_real, precision=highest)
    proj_real = jnp.einsum("ik,cil->ckl", basis_real, prod_real, precision=highest)
    proj_real = proj_real + jnp.einsum("ik,cil->ckl", basis_imag, prod_imag, precision=highest)
    proj_imag = jnp.einsum("ik,cil->ckl", basis_real, prod_imag, precision=highest)
    proj_imag = proj_imag - jnp.einsum("ik,cil->ckl", basis_imag, prod_real, precision=highest)
    projection = jnp.concatenate(
        [proj_real.reshape(chan_owned, -1), proj_imag.reshape(chan_owned, -1)], axis=1
    )
    low_real = basis_real.astype(jnp.bfloat16)
    low_imag = basis_imag.astype(jnp.bfloat16)
    sub_real = jnp.einsum("ik,itc->kct", low_real, full_real, preferred_element_type=jnp.float32)
    sub_real = sub_real + jnp.einsum(
        "ik,itc->kct", low_imag, full_imag, preferred_element_type=jnp.float32
    )
    sub_imag = jnp.einsum("ik,itc->kct", low_real, full_imag, preferred_element_type=jnp.float32)
    sub_imag = sub_imag - jnp.einsum(
        "ik,itc->kct", low_imag, full_real, preferred_element_type=jnp.float32
    )
    owned_power = jnp.sum(sub_real * sub_real + sub_imag * sub_imag, axis=0)
    subspace_power = lax.all_to_all(owned_power, "tm", split_axis=1, concat_axis=0, tiled=True)
    return (covariance, projection, subspace_power)


def solution(mesh):
    return jax.shard_map(
        on_device,
        mesh=mesh,
        in_specs=(P("stn", None, "tm"), P(), P(), P()),
        out_specs=(P(("stn", "tm"), None, None), P(("stn", "tm"), None), P("stn", "tm")),
        check_vma=False,
    )
```

profile of v0, /device:TPU:0, one launch (start us, length us, event | category | flops | bytes accessed | tf_op | source)
XLA Modules:
  0.0 574.7 jit_solution(7616198118002481800)
XLA Ops:
  0.6 4.6 multiply_convert_fusion
  5.3 2.8 reshape.156
  13.2 6.3 %collective-permute-start = (bf16[32,2,15,1024]{3,0,2,1:T(8,128)(2,1)}, bf16[32,2,15,1024]{3,0,2,1:T(8,128)(2,1)}, u32[]{:S(2)}, u32[]{:S(2)}) collective-permute-start(bf16[32,2,15,1024]{3,0,2,1:T(8,128)(2,1)} %copy.85), channel_id=1, source_target_pairs={{0,1},{2,3},{4,5},{6,7},{8,9},{10,11},{12,13},{14,15},{16,17},{18,... | collective-permute-start | bytes 5898248 | tf_op jit(solution)/shard_map/ppermute | solution.py:15
  19.5 8.0 %fusion.40 = bf16[1024,512,1]{1,0,2:T(8,128)(2,1)S(1)} fusion(), kind=kLoop, calls=%fused_computation.88 | loop fusion | flops 8388608 | bytes 1048576 | tf_op jit(solution)/shard_map/convert.6
  27.5 8.6 %negate_convert_fusion = (bf16[1024,512,1]{1,0,2:T(8,128)(2,1)S(1)}, bf16[1024,512,1]{1,0,2:T(8,128)(2,1)S(1)}) fusion(), kind=kLoop, calls=%fused_computation.82 | loop fusion | flops 9961472 | bytes 2097152 | tf_op jit(solution)/shard_map/convert.9
  38.5 6.3 %copy.89 = bf16[1024,512,2]{0,2,1:T(2,128)(2,1)} copy(bf16[1024,512,2]{1,0,2:T(8,128)(2,1)} %get-tuple-element.322) | data formatting | bytes 4194304 | tf_op jit(solution)/shard_map/stack | solution.py:32
  44.8 4.1 convert_element_type.151
  48.9 6.3 %copy.87 = bf16[1024,512,2]{0,2,1:T(2,128)(2,1)} copy(bf16[1024,512,2]{1,0,2:T(8,128)(2,1)} %get-tuple-element.321) | data formatting | bytes 4194304 | tf_op jit(solution)/shard_map/stack | solution.py:31
  55.2 4.1 convert_element_type.150
  60.5 2.6 copy.86
  63.1 12.4 %add_convert_fusion.1 = bf16[32,2,16,1024]{3,2,0,1:T(8,128)(2,1)S(1)} fusion(bf16[32,2,16,1024]{3,2,0,1:T(8,128)(2,1)S(1)} %copy.110, bf16[32,2,15,1024]{3,2,0,1:T(8,128)(2,1)S(1)} %copy.86, f32[1024]{0:T(1024)S(1)} %bitcast.192, f32[1024]{0:T(1024)S(1)} %bitcast.193, f32[1024]{0:T(1024)S(1)} %bitcast.179, f32[1024]{0:T(1024)S(1)} %bitcast.180, ...), kind=kLoop, calls=%fused_computation.51 | loop fusion | flops 97517568 | bytes 6225920 | tf_op jit(solution)/shard_map/convert_element_type | solution.py:103
  78.4 5.1 copy.91
  83.5 6.7 %reshape.157 = bf16[16,2,16384]{2,1,0:T(2,128)(2,1)S(1)} reshape(bf16[1024,16,32]{2,1,0:T(8,128)(2,1)} %bitcast.133) | data formatting | bytes 2097152
  90.2 30.4 %all_to_all.52 = bf16[16,2,16384]{2,1,0:T(2,128)(2,1)S(1)} all-to-all(bf16[16,2,16384]{2,1,0:T(2,128)(2,1)S(1)} %reshape.157), channel_id=1, replica_groups=mesh['stn'=16,'tm'=2] {'stn'}, dimensions={0} | all-to-all | bytes 2097152 | tf_op jit(solution)/shard_map/all_to_all | solution.py:114
  120.6 3.5 reshape.158
  124.1 5.8 %copy.92 = bf16[32,16,16,64]{3,1,0,2:T(8,128)(2,1)S(1)} copy(bf16[32,16,16,64]{0,1,3,2:T(8,128)(2,1)} %bitcast.134) | data formatting | bytes 2097152 | tf_op jit(solution)/shard_map/all_to_all | solution.py:114
  129.9 3.5 copy.93
  133.4 4.1 all-to-all-start.1
  138.2 14.3 %all-to-all-done.1 = bf16[512,16,64]{0,1,2:T(8,128)(2,1)S(1)} async-done(((bf16[512,16,64]{0,1,2:T(8,128)(2,1)}), bf16[512,16,64]{0,1,2:T(8,128)(2,1)S(1)}, u32[]{:S(2)}, u32[]{:S(2)}) %all-to-all-start.1) | async-done | bytes 1048608 | tf_op jit(solution)/shard_map/all_to_all | solution.py:113
  154.0 140.1 %while.14 = (s32[]{:T(128)}, f32[16,512,1024]{1,2,0:T(8,128)}, bf16[512,32,16]{0,2,1:T(8,128)(2,1)S(1)}, bf16[512,32,16]{0,2,1:T(8,128)(2,1)S(1)}, s32[]{:T(128)}, /*index=5*/s32[]{:T(128)}, s32[]{:T(128)}, s32[]{:T(128)}) while((s32[]{:T(128)}, f32[16,512,1024]{1,2,0:T(8,128)}, bf16[512,32,16]{0,2,1:T(8,128)(2,1)S(1)}, ...), condition=%wide.region_1.2_spmd.clone, body=%wide.region_0.1_spmd.clone.sunk | while | flops 612368384 | bytes 203948176 | solution.py:81
  154.1 8.5 %fusion.105 = f32[16,512,512]{1,2,0:T(8,128)} fusion(bf16[512,16,16]{0,2,1:T(8,128)(2,1)S(1)} %get-tuple-element.387), kind=kOutput, calls=%fused_computation.10.clone.1 | convolution fusion | flops 134217728 | bytes 17039360 | tf_op jit(solution)/shard_map/while/body/eval_jaxpr/itc,jtc->cij/dot_general | solution.py:56
  162.7 8.1 %add_convert_fusion.4 = bf16[16,512,512]{1,2,0:T(8,128)(2,1)S(1)} fusion(f32[16,512,512]{1,2,0:T(8,128)} %fusion.105, bf16[512,16,16]{0,2,1:T(8,128)(2,1)S(1)} %get-tuple-element.386), kind=kOutput, calls=%fused_computation.3.clone.1 | convolution fusion | flops 142606336 | bytes 25427968 | tf_op jit(solution)/shard_map/while/body/eval_jaxpr/itc,jtc->cij/dot_general | solution.py:57
  170.8 8.5 %fusion.104 = f32[16,512,512]{1,2,0:T(8,128)} fusion(bf16[512,16,16]{0,2,1:T(8,128)(2,1)S(1)} %get-tuple-element.386, bf16[512,16,16]{0,2,1:T(8,128)(2,1)S(1)} %get-tuple-element.387), kind=kOutput, calls=%fused_computation.5.clone.1 | convolution fusion | flops 134217728 | bytes 17301504 | tf_op jit(solution)/shard_map/while/body/eval_jaxpr/itc,jtc->cij/dot_general | solution.py:60
  179.4 11.4 %subtract_convert_fusion.2 = bf16[16,512,512]{1,2,0:T(8,128)(2,1)} fusion(f32[16,512,512]{1,2,0:T(8,128)} %fusion.104, bf16[512,16,16]{0,2,1:T(8,128)(2,1)S(1)} %get-tuple-element.386, bf16[512,16,16]{0,2,1:T(8,128)(2,1)S(1)} %get-tuple-element.387), kind=kOutput, calls=%fused_computation.2.clone.1 | convolution fusion | flops 142606336 | bytes 25690112 | tf_op jit(solution)/shard_map/while/body/eval_jaxpr/itc,jtc->cij/dot_general | solution.py:61
  190.7 10.3 %pad_maximum_fusion.6 = bf16[16,512,1024]{1,2,0:T(8,128)(2,1)} fusion(bf16[16,512,512]{1,2,0:T(8,128)(2,1)} %subtract_convert_fusion.2, bf16[16,512,512]{1,2,0:T(8,128)(2,1)S(1)} %add_convert_fusion.4), kind=kLoop, calls=%fused_computation.1.clone.1 | loop fusion | flops 33554432 | bytes 33554432 | tf_op jit(solution)/shard_map/while/body/eval_jaxpr/concatenate | solution.py:76
  201.0 19.1 %select_add_fusion.2 = f32[16,512,1024]{1,2,0:T(8,128)} fusion(f32[16,512,1024]{1,2,0:T(8,128)} %get-tuple-element.397, bf16[16,512,1024]{1,2,0:T(8,128)(2,1)} %pad_maximum_fusion.6, pred[]{:T(512)S(6)} %compare.19), kind=kLoop, calls=%fused_computation.clone.1 | loop fusion | flops 25165824 | bytes 83886080 | tf_op jit(solution)/shard_map/while/body/eval_jaxpr/add | solution.py:78
  220.1 8.5 %fusion.105 = f32[16,512,512]{1,2,0:T(8,128)} fusion(bf16[512,16,16]{0,2,1:T(8,128)(2,1)S(1)} %get-tuple-element.387), kind=kOutput, calls=%fused_computation.10.clone.1 | convolution fusion | flops 134217728 | bytes 17039360 | tf_op jit(solution)/shard_map/while/body/eval_jaxpr/itc,jtc->cij/dot_general | solution.py:56
  228.7 8.2 %add_convert_fusion.4 = bf16[16,512,512]{1,2,0:T(8,128)(2,1)S(1)} fusion(f32[16,512,512]{1,2,0:T(8,128)} %fusion.105, bf16[512,16,16]{0,2,1:T(8,128)(2,1)S(1)} %get-tuple-element.386), kind=kOutput, calls=%fused_computation.3.clone.1 | convolution fusion | flops 142606336 | bytes 25427968 | tf_op jit(solution)/shard_map/while/body/eval_jaxpr/itc,jtc->cij/dot_general | solution.py:57
  236.8 8.5 %fusion.104 = f32[16,512,512]{1,2,0:T(8,128)} fusion(bf16[512,16,16]{0,2,1:T(8,128)(2,1)S(1)} %get-tuple-element.386, bf16[512,16,16]{0,2,1:T(8,128)(2,1)S(1)} %get-tuple-element.387), kind=kOutput, calls=%fused_computation.5.clone.1 | convolution fusion | flops 134217728 | bytes 17301504 | tf_op jit(solution)/shard_map/while/body/eval_jaxpr/itc,jtc->cij/dot_general | solution.py:60
  245.4 11.4 %subtract_convert_fusion.2 = bf16[16,512,512]{1,2,0:T(8,128)(2,1)} fusion(f32[16,512,512]{1,2,0:T(8,128)} %fusion.104, bf16[512,16,16]{0,2,1:T(8,128)(2,1)S(1)} %get-tuple-element.386, bf16[512,16,16]{0,2,1:T(8,128)(2,1)S(1)} %get-tuple-element.387), kind=kOutput, calls=%fused_computation.2.clone.1 | convolution fusion | flops 142606336 | bytes 25690112 | tf_op jit(solution)/shard_map/while/body/eval_jaxpr/itc,jtc->cij/dot_general | solution.py:61
  256.7 10.3 %pad_maximum_fusion.6 = bf16[16,512,1024]{1,2,0:T(8,128)(2,1)} fusion(bf16[16,512,512]{1,2,0:T(8,128)(2,1)} %subtract_convert_fusion.2, bf16[16,512,512]{1,2,0:T(8,128)(2,1)S(1)} %add_convert_fusion.4), kind=kLoop, calls=%fused_computation.1.clone.1 | loop fusion | flops 33554432 | bytes 33554432 | tf_op jit(solution)/shard_map/while/body/eval_jaxpr/concatenate | solution.py:76
  267.0 27.2 %select_add_fusion.2 = f32[16,512,1024]{1,2,0:T(8,128)} fusion(f32[16,512,1024]{1,2,0:T(8,128)} %get-tuple-element.397, bf16[16,512,1024]{1,2,0:T(8,128)(2,1)} %pad_maximum_fusion.6, pred[]{:T(512)S(6)} %compare.19), kind=kLoop, calls=%fused_computation.clone.1 | loop fusion | flops 25165824 | bytes 83886080 | tf_op jit(solution)/shard_map/while/body/eval_jaxpr/add | solution.py:78
  294.2 31.9 %copy.100 = f32[16,512,1024]{2,1,0:T(8,128)} copy(f32[16,512,1024]{1,2,0:T(8,128)} %get-tuple-element.82) | data formatting | bytes 67108864 | tf_op jit(solution)/shard_map/while | solution.py:81
  326.1 19.0 %broadcast_multiply_fusion = (f32[16,512,1024]{2,1,0:T(8,128)S(1)}, bf16[16,512,1024]{2,1,0:T(8,128)(2,1)}) fusion(f32[16,512,1024]{2,1,0:T(8,128)} %copy.100), kind=kLoop, calls=%fused_computation.14 | loop fusion | flops 16777216 | bytes 83886080 | tf_op jit(solution)/shard_map/div | solution.py:125
  345.1 11.4 %copy-done = f32[16,512,1024]{2,1,0:T(8,128)} copy-done((f32[16,512,1024]{2,1,0:T(8,128)}, f32[16,512,1024]{2,1,0:T(8,128)S(1)}, u32[]{:S(2)}) %copy-start) | copy-done | bytes 33554456
  357.9 40.0 %psum.7 = bf16[2,512,8]{1,2,0:T(8,128)(2,1)S(1)} all-reduce(bf16[2,512,8]{1,2,0:T(8,128)(2,1)S(1)} %maximum_select_fusion), channel_id=1, replica_groups=mesh['stn'=16,'tm'=2] {'stn','tm'}, use_global_device_ids=true, to_apply=%region_2.3 | all-reduce | flops 8192 | bytes 32768 | tf_op jit(solution)/shard_map/psum | solution.py:20
  402.5 7.9 %add_reduce_fusion.6 = (f32[]{:T(128)}, f32[]{:T(128)}, f32[]{:T(128)}, f32[]{:T(128)}, f32[]{:T(128)}, /*index=5*/f32[]{:T(128)}, f32[]{:T(128)}, f32[]{:T(128)...) fusion(f32[512]{0:T(512)S(1)} %bitcast.173, ...), kind=kLoop, calls=%fused_computation.163 | loop fusion | flops 50164 | bytes 61540 | tf_op jit(solution)/shard_map/reduce_sum | solution.py:45
  413.0 6.9 %add_reduce_fusion.5 = (f32[]{:T(128)}, f32[]{:T(128)}, f32[]{:T(128)}, f32[]{:T(128)}, f32[]{:T(128)}, /*index=5*/f32[]{:T(128)}, f32[]{:T(128)}, f32[]{:T(128)...) fusion(f32[512]{0:T(512)S(1)} %get-tuple-element.300, ...), kind=kLoop, calls=%fused_computation.159 | loop fusion | flops 41974 | bytes 53332 | tf_op jit(solution)/shard_map/reduce_sum | solution.py:45
  422.6 5.8 %add_reduce_fusion.4 = (f32[]{:T(128)}, f32[]{:T(128)}, f32[]{:T(128)}, f32[]{:T(128)}, f32[]{:T(128)}, /*index=5*/f32[]{:T(128)}, f32[]{:T(128)}, f32[]{:T(128)...) fusion(f32[512]{0:T(512)S(1)} %get-tuple-element.285, ...), kind=kLoop, calls=%fused_computation.155 | loop fusion | flops 33784 | bytes 45124 | tf_op jit(solution)/shard_map/reduce_sum | solution.py:45
  430.8 4.5 add_reduce_fusion.3
  437.9 3.3 add_reduce_fusion.2
  448.3 35.0 %subtract_multiply_fusion = (f32[512,1]{0,1:T(1,128)S(1)}, f32[512,1]{0,1:T(1,128)S(1)}, f32[512,1]{0,1:T(1,128)S(1)}, f32[512,1]{0,1:T(1,128)S(1)}, f32[512,1]{...) fusion(f32[512,1]{0,1:T(1,128)S(1)} %get-tuple-element.342, ...), kind=kLoop, calls=%fused_computation.138 | loop fusion | flops 107008 | bytes 57596 | tf_op jit(solution)/shard_map/mul | solution.py:51
  483.2 9.0 %subtract_multiply_fusion.1 = f32[512,1]{0,1:T(1,128)S(1)} fusion(f32[512,1]{0,1:T(1,128)S(1)} %get-tuple-element.235, f32[512,1]{0,1:T(1,128)S(1)} %get-tuple-element.236, f32[512,1]{0,1:T(1,128)S(1)} %get-tuple-element.237, f32[512,1]{0,1:T(1,128)S(1)} %get-tuple-element.238, f32[512,1]{0,1:T(1,128)S(1)} %get-tuple-element.239, ...), kind=kLoop, calls=%fused_computation.140 | loop fusion | flops 14848 | bytes 32828 | tf_op jit(solution)/shard_map/mul | solution.py:50
  493.8 17.6 %fusion.8 = f32[16,512,8]{1,2,0:T(8,128)S(1)} fusion(f32[16,512,1024]{2,1,0:T(8,128)} %copy-done, f32[512,8]{0,1:T(8,128)S(1)} %stack.24), kind=kOutput, calls=%fused_computation.15 | convolution fusion | flops 402653184 | bytes 17055744 | tf_op jit(solution)/shard_map/cij,jk->cik/dot_general | solution.py:149
  511.4 17.6 %fusion.10 = f32[16,512,8]{1,2,0:T(8,128)S(1)} fusion(f32[16,512,1024]{2,1,0:T(8,128)} %copy-done, f32[512,8]{0,1:T(8,128)S(1)} %stack.25), kind=kOutput, calls=%fused_computation.17 | convolution fusion | flops 402653184 | bytes 17055744 | tf_op jit(solution)/shard_map/cij,jk->cik/dot_general | solution.py:147
  531.2 3.5 all-to-all-start.2
  534.8 17.7 %fusion.43 = f32[16,512,8]{1,2,0:T(8,128)S(1)} fusion(f32[16,512,8]{1,2,0:T(8,128)S(1)} %fusion.10, f32[16,512,1024]{2,1,0:T(8,128)} %copy-done, f32[512,8]{0,1:T(8,128)S(1)} %stack.24), kind=kOutput, calls=%fused_computation.89 | convolution fusion | flops 402718720 | bytes 17317888 | tf_op jit(solution)/shard_map/cij,jk->cik/dot_general | solution.py:146
  552.9 17.6 %fusion.46 = f32[16,512,8]{1,2,0:T(8,128)S(1)} fusion(f32[16,512,8]{1,2,0:T(8,128)S(1)} %fusion.8, f32[16,512,1024]{2,1,0:T(8,128)} %copy-done, f32[512,8]{0,1:T(8,128)S(1)} %stack.25), kind=kOutput, calls=%fused_computation.90 | convolution fusion | flops 402718720 | bytes 17317888 | tf_op jit(solution)/shard_map/cij,jk->cik/dot_general | solution.py:148
  (72 shorter events, 39.2 us)
Async XLA Ops:
  13.2 47.2 %collective-permute-start = (bf16[32,2,15,1024]{3,0,2,1:T(8,128)(2,1)}, bf16[32,2,15,1024]{3,0,2,1:T(8,128)(2,1)}, u32[]{:S(2)}, u32[]{:S(2)}) collective-permute-start(bf16[32,2,15,1024]{3,0,2,1:T(8,128)(2,1)} %copy.85), channel_id=1, source_target_pairs={{0,1},{2,3},{4,5},{6,7},{8,9},{10,11},{12,13},{14,15},{16,17},{18,... | collective-permute-start | bytes 5898248 | tf_op jit(solution)/shard_map/ppermute | solution.py:15
  48.9 10.4 %copy-start.7 = (f32[16,1024]{1,0:T(8,128)S(1)}, f32[16,1024]{1,0:T(8,128)}, u32[]{:S(2)}) copy-start(f32[16,1024]{1,0:T(8,128)} %param.7) | copy-start | bytes 196612
  63.1 12.4 %copy-start.3 = (bf16[1024,1024]{0,1:T(8,128)(2,1)S(1)}, bf16[1024,1024]{0,1:T(8,128)(2,1)}, u32[]{:S(2)}) copy-start(bf16[1024,1024]{0,1:T(8,128)(2,1)} %convert_element_type.151) | copy-start | bytes 6291460
  75.5 1.6 copy-start.4
  133.4 19.2 %all-to-all-start.1 = ((bf16[512,16,64]{0,1,2:T(8,128)(2,1)}), bf16[512,16,64]{0,1,2:T(8,128)(2,1)S(1)}, u32[]{:S(2)}, u32[]{:S(2)}) async-start(bf16[512,16,64]{0,1,2:T(8,128)(2,1)} %copy.93), calls=%async_computation.1 | async-start | bytes 2097152 | tf_op jit(solution)/shard_map/all_to_all | solution.py:113
  152.8 0.8 copy-start.1
  152.8 1.0 copy-start.5
  345.0 11.5 %copy-start = (f32[16,512,1024]{2,1,0:T(8,128)}, f32[16,512,1024]{2,1,0:T(8,128)S(1)}, u32[]{:S(2)}) copy-start(f32[16,512,1024]{2,1,0:T(8,128)S(1)} %get-tuple-element.317) | copy-start | bytes 100663296
  345.1 11.6 %copy-start.8 = (s32[8]{0:T(128)S(1)}, s32[8]{0:T(128)}, u32[]{:S(2)}) copy-start(s32[8]{0:T(128)} %param.9) | copy-start | bytes 100
  345.1 147.3 %copy-start.2 = (bf16[512,32,16,1]{0,1,3,2:T(8,128)(2,1)S(1)}, bf16[512,32,16,1]{0,1,3,2:T(8,128)(2,1)}, u32[]{:S(2)}) copy-start(bf16[512,32,16,1]{0,1,3,2:T(8,128)(2,1)} %copy-done.1) | copy-start | bytes 1572868
  345.1 148.0 %copy-start.6 = (bf16[512,32,16,1]{0,1,3,2:T(8,128)(2,1)S(1)}, bf16[512,32,16,1]{0,1,3,2:T(8,128)(2,1)}, u32[]{:S(2)}) copy-start(bf16[512,32,16,1]{0,1,3,2:T(8,128)(2,1)} %copy-done.5) | copy-start | bytes 1572868
  531.2 41.3 %all-to-all-start.2 = ((f32[2,1,256]{2,1,0:T(1,128)}), f32[2,1,256]{2,1,0:T(1,128)S(1)}, u32[]{:S(2)}, u32[]{:S(2)}) async-start(f32[2,1,256]{2,1,0:T(1,128)} %reshape.159), calls=%async_computation.2 | async-start | bytes 4096 | tf_op jit(solution)/shard_map/all_to_all | solution.py:168
where the time goes:
time: 582 us; the launch traced here: 575 us
  other arithmetic  212 us (36%)
  matrix products  152 us (26%)
  local copies, waits for them, and re-layouts  104 us (18%)
  blocking collectives  70.4 us (12%)
  waiting for transfers between devices  15.4 us (3%)
  starting transfers between devices  14 us (2%)
  between operations  7.33 us (1%)
    add x2, other arithmetic, add_block(): return total + rounded  46.3 us
    psum x1, blocking collectives, spread(): return lax.psum(jnp.where(mine, shard, jnp.zeros_like(shard)), axis)  40 us
    mul x1, other arithmetic, orthonormal(): basis_imag.append(vec_imag * inverse)  35 us
    while x1, local copies, waits for them, and re-layouts, blockwise_covariance(): return lax.fori_loop(0, blocks, add_block, start)  31.9 us
    reduce_sum x7, other arithmetic, orthonormal(): inner_real = jnp.sum(q_real * vec_real + q_imag * vec_imag)  30.9 us
    all_to_all x1, blocking collectives, on_device(): lax.all_to_all(spectra, 'stn', split_axis=2, concat_axis=0, tiled=True)  30.4 us
    unnamed x24, local copies, waits for them, and re-layouts  23.9 us
    dot_general x2, matrix products, block_sums(): jnp.einsum('itc,jtc->cij', part_real, part_imag, preferred_element_type=j...  22.7 us
  transfers between devices with their start and end apart: 3, of which 2 were waited for; matrix products, arithmetic and copies ran while one was open for 13% of the time, Pallas kernels for 0%

commit v1 on v0

--- a/solution.py
+++ b/solution.py
@@ -1,8 +1,11 @@
+import functools
 import math
 
 import jax
 import jax.numpy as jnp
 from jax import lax
+from jax.experimental import pallas as pl
+from jax.experimental.pallas import tpu as pltpu
 from jax.sharding import PartitionSpec as P
 
 NFFT = 1024
@@ -81,7 +84,7 @@
     return lax.fori_loop(0, blocks, add_block, start)
 
 
-def on_device(voltages, filter_taps, reference_channel, basis_inputs):
+def plain_plan(voltages, filter_taps, reference_channel, basis_inputs):
     blocks = lax.axis_size("tm")
     local_inputs = voltages.shape[0]
     inputs_all = local_inputs * lax.axis_size("stn")
@@ -169,6 +172,381 @@
     return (covariance, projection, subspace_power)
 
 
+LANES = 128
+SUB = 8
+ROWS = 16
+NT_DIMS = (((1,), (1,)), ((), ()))
+
+
+def nt_dot(a, b, precision=None):
+    return lax.dot_general(a, b, NT_DIMS, precision=precision, preferred_element_type=jnp.float32)
+
+
+class Plan:
+    def __init__(self, voltages, filter_taps):
+        self.blocks = lax.axis_size("tm")
+        self.devices = lax.axis_size("stn") * self.blocks
+        self.taps, self.nfft = filter_taps.shape
+        self.chans = self.nfft // 2 // self.devices
+        self.inputs = voltages.shape[0] // self.blocks
+        self.inputs_all = voltages.shape[0] * lax.axis_size("stn")
+        self.frames = voltages.shape[2] // self.nfft
+        self.spectra = self.frames * self.blocks
+        self.tiles = 2 * self.nfft // LANES
+        self.group = LANES // self.spectra
+        self.quads = self.chans // max(self.group, 1)
+        self.chunk = 2 * self.quads * self.inputs
+        self.extra = self.inputs // 2
+
+    def packed(self):
+        return (
+            self.blocks == 2
+            and self.group == 4
+            and self.group * self.spectra == LANES
+            and 2 * self.quads == SUB
+            and self.inputs == ROWS
+            and self.tiles == ROWS
+        )
+
+
+def table_kernel(plan, rows, out_ref):
+    shape = (rows, LANES)
+    row = lax.broadcasted_iota(jnp.int32, shape, 0) + pl.program_id(0) * rows
+    lane = lax.broadcasted_iota(jnp.int32, shape, 1)
+    per_dest = plan.group * 2 * plan.quads
+    dest = lax.div(row, per_dest)
+    member = lax.rem(lax.div(row, 2 * plan.quads), plan.group)
+    part = lax.rem(lax.div(row, plan.quads), 2)
+    quad = lax.rem(row, plan.quads)
+    channel = dest * plan.chans + quad * plan.group + member
+    unit = 2.0 * math.pi / plan.nfft
+    phase = lax.rem(lane * channel + part * (plan.nfft // 4), plan.nfft)
+    angle = phase.astype(jnp.float32) * unit
+    factor = 1.0 / math.sqrt(plan.nfft)
+    cosine = jnp.cos(angle) * factor
+    sine = jnp.sin(angle) * factor
+    turn = lax.rem(channel * LANES, plan.nfft).astype(jnp.float32) * unit
+    turn_cos = jnp.cos(turn)
+    turn_sin = jnp.sin(turn)
+    for tile in range(plan.nfft // LANES):
+        first = 2 * tile * LANES
+        out_ref[:, first : first + LANES] = cosine.astype(jnp.bfloat16)
+        out_ref[:, first + LANES : first + 2 * LANES] = sine.astype(jnp.bfloat16)
+        cosine, sine = (
+            cosine * turn_cos - sine * turn_sin,
+            sine * turn_cos + cosine * turn_sin,
+        )
+
+
+def transform_table(plan):
+    rows = 128
+    total = plan.nfft
+    return pl.pallas_call(
+        functools.partial(table_kernel, plan, rows),
+        grid=(total // rows,),
+        out_specs=pl.BlockSpec((rows, 2 * plan.nfft), lambda r: (r, 0)),
+        out_shape=jax.ShapeDtypeStruct((total, 2 * plan.nfft), jnp.bfloat16),
+        name="table",
+    )()
+
+
+def lane_iota(rows):
+    return lax.broadcasted_iota(jnp.int32, (rows, LANES), 1)
+
+
+def regroup(values):
+    lane = lane_iota(SUB)
+    low = lane < 64
+    even = (lane & 32) == 0
+    v0, v1, v2, v3 = values
+    x0 = jnp.where(low, v0, pltpu.roll(v2, 64, 1))
+    y0 = jnp.where(low, pltpu.roll(v0, 64, 1), v2)
+    x1 = jnp.where(low, v1, pltpu.roll(v3, 64, 1))
+    y1 = jnp.where(low, pltpu.roll(v1, 64, 1), v3)
+    out = []
+    for a, b in ((x0, x1), (y0, y1)):
+        out.append(jnp.where(even, a, pltpu.roll(b, 32, 1)))
+        out.append(jnp.where(even, pltpu.roll(a, 96, 1), b))
+    return out
+
+
+def channelize_kernel(
+    plan, half, where_ref, own_ref, recv_ref, taps_ref, table_hbm, out_ref, table, sig, filt, low, prod, spread_f32, sem
+):
+    step = pl.program_id(0)
+    block = where_ref[0]
+    copy = pltpu.make_async_copy(table_hbm, table, sem)
+
+    @pl.when(step == 0)
+    def _():
+        copy.start()
+
+    frames, spectra, taps = plan.frames, plan.spectra, plan.taps
+    span = frames * ROWS
+
+    def one_input(i, carry):
+        own_at = pl.multiple_of(block * span, span)
+        recv_at = pl.multiple_of((1 - block) * span, span)
+        start = pl.multiple_of(i * span, span)
+        sig[pl.ds(own_at, span), :] = own_ref[pl.ds(start, span), :].astype(jnp.float32)
+        sig[pl.ds(recv_at, span), :] = recv_ref[pl.ds(start, span), :].astype(jnp.float32)
+        base = pl.multiple_of(i * (spectra * ROWS), spectra * ROWS)
+        for sub in range(ROWS // SUB):
+            tap = [taps_ref[k * ROWS + sub * SUB : k * ROWS + (sub + 1) * SUB, :] for k in range(taps)]
+            data = [sig[f * ROWS + sub * SUB : f * ROWS + (sub + 1) * SUB, :] for f in range(spectra)]
+            for t in range(spectra):
+                acc = None
+                for k in range(max(0, taps - 1 - t), taps):
+                    term = tap[k] * data[t - (taps - 1) + k]
+                    acc = term if acc is None else acc + term
+                filt[pl.ds(base + t * ROWS + sub * SUB, SUB), :] = acc
+        return carry
+
+    lax.fori_loop(0, half, one_input, 0)
+    for tile in range(plan.tiles):
+        picked = filt[pl.ds(tile, half * spectra, stride=ROWS), :]
+        low[:, tile * LANES : (tile + 1) * LANES] = picked.astype(jnp.bfloat16)
+
+    @pl.when(step == 0)
+    def _():
+        copy.wait()
+
+    prod[...] = nt_dot(table[...], low[...])
+    per_dest = plan.group * SUB
+
+    def one_dest(d, carry):
+        rows = pl.multiple_of(d * per_dest, per_dest)
+        for part in range(half // plan.group):
+            cols = slice(part * LANES, (part + 1) * LANES)
+            moved = regroup([prod[pl.ds(rows + c * SUB, SUB), cols] for c in range(plan.group)])
+            for b in range(plan.group):
+                at = d * (SUB * ROWS) + step * half + part * plan.group + b
+                spread_f32[pl.ds(at, SUB, stride=ROWS), :] = moved[b]
+        return carry
+
+    lax.fori_loop(0, plan.devices, one_dest, 0)
+
+    @pl.when(step == pl.num_programs(0) - 1)
+    def _():
+        channel = where_ref[1]
+        owner = lax.div(channel, plan.chans)
+        local = lax.rem(channel, plan.chans)
+        quad = lax.div(local, plan.group)
+        member = lax.rem(local, plan.group)
+        lane = lane_iota(ROWS)
+        tiles = []
+        for part in range(2):
+            at = pl.multiple_of((owner * SUB + part * plan.quads + quad) * ROWS, ROWS)
+            tiles.append(spread_f32[pl.ds(at, ROWS), :])
+        shift = LANES - member * plan.spectra
+        real = pltpu.roll(tiles[0], lax.rem(shift, LANES), 1)
+        imag = pltpu.roll(tiles[1], lax.rem(shift + plan.spectra, LANES), 1)
+        both = jnp.where(lane < plan.spectra, real, imag)
+        folded = jnp.where(lane_iota(SUB) < 64, both[:SUB], pltpu.roll(both[SUB:], 64, 1))
+        folded = folded.astype(jnp.bfloat16)
+
+        def finish(d, carry):
+            at = pl.multiple_of(d * plan.chunk, plan.chunk)
+            out_ref[d, : plan.chunk, :] = spread_f32[pl.ds(at, plan.chunk), :].astype(jnp.bfloat16)
+            out_ref[d, plan.chunk :, :] = folded
+            return carry
+
+        lax.fori_loop(0, plan.devices, finish, 0)
+
+
+def channelize(plan, where, own, recv, taps, table):
+    half = plan.inputs // 2
+    rows = half * plan.frames * ROWS
+    out = (plan.devices, plan.chunk + plan.extra, LANES)
+    return pl.pallas_call(
+        functools.partial(channelize_kernel, plan, half),
+        grid_spec=pltpu.PrefetchScalarGridSpec(
+            num_scalar_prefetch=1,
+            grid=(2,),
+            in_specs=[
+                pl.BlockSpec((rows, LANES), lambda g, w: (w[0] * 2 + g, 0)),
+                pl.BlockSpec((rows, LANES), lambda g, w: (g, 0)),
+                pl.BlockSpec(taps.shape, lambda g, w: (0, 0)),
+                pl.BlockSpec(memory_space=pl.ANY),
+            ],
+            out_specs=pl.BlockSpec(out, lambda g, w: (0, 0, 0)),
+            scratch_shapes=[
+                pltpu.VMEM(table.shape, jnp.bfloat16),
+                pltpu.VMEM((plan.spectra * ROWS, LANES), jnp.float32),
+                pltpu.VMEM((half * plan.spectra * ROWS, LANES), jnp.float32),
+                pltpu.VMEM((half * plan.spectra, 2 * plan.nfft), jnp.bfloat16),
+                pltpu.VMEM((plan.nfft, half * plan.spectra), jnp.float32),
+                pltpu.VMEM((plan.devices * plan.chunk, LANES), jnp.float32),
+                pltpu.SemaphoreType.DMA(()),
+            ],
+        ),
+        out_shape=jax.ShapeDtypeStruct(out, jnp.bfloat16),
+        name="channelize",
+    )(where, own, recv, taps, table)
+
+
+def pair_of(recv_ref, plan, quad):
+    shape = (plan.inputs_all, LANES)
+    real = recv_ref[:, quad * ROWS : (quad + 1) * ROWS, :].reshape(shape)
+    at = (plan.quads + quad) * ROWS
+    imag = recv_ref[:, at : at + ROWS, :].reshape(shape)
+    return real, imag
+
+
+def inverse_root(value):
+    y = lax.rsqrt(value)
+    return y * (1.5 - 0.5 * value * y * y)
+
+
+def basis_kernel(plan, count, recv_ref, picks_ref, proj_ref, power_ref):
+    highest = lax.Precision.HIGHEST
+    span = plan.spectra
+    folded = recv_ref[:, plan.chunk :, :].astype(jnp.float32)
+    turned = pltpu.roll(folded.reshape(-1, LANES), 64, 1).reshape(folded.shape)
+    ref = jnp.concatenate([folded, turned], axis=1).reshape(plan.inputs_all, LANES)
+    ref = ref.astype(jnp.bfloat16)
+    rows = lax.broadcasted_iota(jnp.int32, (count, plan.inputs_all), 1)
+    onehot = (rows == picks_ref[...]).astype(jnp.float32).astype(jnp.bfloat16)
+    chosen = jnp.dot(onehot, ref, preferred_element_type=jnp.float32)
+    lane = lane_iota(count)
+    zero = jnp.zeros_like(chosen)
+    left = jnp.where(lane < 2 * span, chosen, zero)
+    cross = jnp.where(
+        lane < span,
+        -pltpu.roll(chosen, LANES - span, 1),
+        jnp.where(lane < 2 * span, pltpu.roll(chosen, span, 1), zero),
+    )
+    real = nt_dot(left.astype(jnp.bfloat16), ref) / span
+    imag = nt_dot(cross.astype(jnp.bfloat16), ref) / span
+    index = lax.broadcasted_iota(jnp.int32, real.shape, 0)
+    for j in range(count):
+        vr = jnp.broadcast_to(real[j : j + 1], real.shape)
+        vi = jnp.broadcast_to(imag[j : j + 1], real.shape)
+        inner_r = jnp.sum(vr * real + vi * imag, axis=1, keepdims=True)
+        inner_i = jnp.sum(vr * imag - vi * real, axis=1, keepdims=True)
+        inverse = inverse_root(inner_r[j : j + 1] + 1e-06)
+        qr = vr * inverse
+        qi = vi * inverse
+        inner_r = inner_r * inverse
+        inner_i = inner_i * inverse
+        later = index > j
+        this = index == j
+        next_r = real - (qr * inner_r - qi * inner_i)
+        next_i = imag - (qr * inner_i + qi * inner_r)
+        real = jnp.where(this, qr, jnp.where(later, next_r, real))
+        imag = jnp.where(this, qi, jnp.where(later, next_i, imag))
+    levels = []
+    rest_r, rest_i = real, imag
+    for _ in range(3):
+        top_r = rest_r.astype(jnp.bfloat16).astype(jnp.float32)
+        top_i = rest_i.astype(jnp.bfloat16).astype(jnp.float32)
+        levels += [top_r, top_i]
+        rest_r = rest_r - top_r
+        rest_i = rest_i - top_i
+    stack = jnp.concatenate(levels, axis=0).astype(jnp.bfloat16)
+    members = plan.group * count
+    row = lax.broadcasted_iota(jnp.int32, (members, LANES), 0)
+    col = lax.broadcasted_iota(jnp.int32, (members, LANES), 1)
+    mine = lax.div(row, count) == lax.div(col, span)
+    size = count * count
+    lead = lax.broadcasted_iota(jnp.int32, (count, 2 * size), 0)
+    spot = lax.broadcasted_iota(jnp.int32, (count, 2 * size), 1)
+    fits = lax.rem(spot, count) == lead
+    put_r = jnp.where(fits & (spot < size), 1.0, 0.0)
+    put_i = jnp.where(fits & (spot >= size), 1.0, 0.0)
+    wide = lax.broadcasted_iota(jnp.int32, (members, 2 * size), 1)
+    tall = lax.broadcasted_iota(jnp.int32, (members, 2 * size), 0)
+    keep = lax.rem(lax.div(wide, count), count) == lax.rem(tall, count)
+    for quad in range(plan.quads):
+        xr, xi = pair_of(recv_ref, plan, quad)
+        sr = jnp.dot(stack, xr, preferred_element_type=jnp.float32)
+        si = jnp.dot(stack, xi, preferred_element_type=jnp.float32)
+        piece = lambda s, n: s[n * count : (n + 1) * count]
+        low_r = piece(sr, 0) + piece(si, 1)
+        low_i = piece(si, 0) - piece(sr, 1)
+        power_ref[quad : quad + 1, :] = jnp.sum(low_r * low_r + low_i * low_i, axis=0, keepdims=True)
+        yr = low_r + ((piece(sr, 2) + piece(si, 3)) + (piece(sr, 4) + piece(si, 5)))
+        yi = low_i + ((piece(si, 2) - piece(sr, 3)) + (piece(si, 4) - piece(sr, 5)))
+        tiled_r = jnp.where(mine, jnp.concatenate([yr] * plan.group, axis=0), 0.0)
+        tiled_i = jnp.where(mine, jnp.concatenate([yi] * plan.group, axis=0), 0.0)
+        both = jnp.concatenate([yr, yi], axis=1)
+        left_r = jnp.concatenate([tiled_r, tiled_i], axis=1)
+        left_i = jnp.concatenate([tiled_i, -tiled_r], axis=1)
+        gram_r = nt_dot(left_r, both, highest) / span
+        gram_i = nt_dot(left_i, both, highest) / span
+        placed = jnp.dot(gram_r, put_r, precision=highest) + jnp.dot(gram_i, put_i, precision=highest)
+        placed = jnp.where(keep, placed, 0.0).reshape(plan.group, count, 2 * size)
+        proj_ref[quad * plan.group : (quad + 1) * plan.group, :] = jnp.sum(placed, axis=1)
+
+
+def subspace(plan, recv, basis_inputs):
+    count = basis_inputs.shape[0]
+    return pl.pallas_call(
+        functools.partial(basis_kernel, plan, count),
+        out_shape=(
+            jax.ShapeDtypeStruct((plan.chans, 2 * count * count), jnp.float32),
+            jax.ShapeDtypeStruct((plan.quads, LANES), jnp.float32),
+        ),
+        name="subspace",
+    )(recv, basis_inputs.reshape(count, 1))
+
+
+def covariance_kernel(plan, real_ref, imag_ref, out_ref):
+    member = lax.rem(pl.program_id(0), plan.group)
+    shape = (plan.inputs_all, LANES)
+    real = real_ref[...].reshape(shape)
+    imag = imag_ref[...].reshape(shape)
+    inside = lax.div(lax.broadcasted_iota(jnp.int32, (1, LANES), 1), plan.spectra) == member
+    mask = jnp.where(inside, 1.0 / plan.spectra, 0.0).astype(jnp.bfloat16)
+    left_r = real * mask
+    left_i = imag * mask
+    right = jnp.concatenate([real, imag], axis=1)
+    total = plan.inputs_all
+    out_ref[0, :, :total] = nt_dot(jnp.concatenate([left_r, left_i], axis=1), right).astype(jnp.bfloat16)
+    out_ref[0, :, total:] = nt_dot(jnp.concatenate([left_i, -left_r], axis=1), right).astype(jnp.bfloat16)
+
+
+def covariances(plan, recv):
+    out = (plan.chans, plan.inputs_all, 2 * plan.inputs_all)
+    block = (plan.devices, ROWS, LANES)
+    return pl.pallas_call(
+        functools.partial(covariance_kernel, plan),
+        grid=(plan.chans,),
+        in_specs=[
+            pl.BlockSpec(block, lambda c: (0, c // plan.group, 0)),
+            pl.BlockSpec(block, lambda c: (0, plan.quads + c // plan.group, 0)),
+        ],
+        out_specs=pl.BlockSpec((1, *out[1:]), lambda c: (c, 0, 0)),
+        out_shape=jax.ShapeDtypeStruct(out, jnp.bfloat16),
+        name="covariance",
+    )(recv, recv)
+
+
+def packed_plan(plan, voltages, filter_taps, reference_channel, basis_inputs):
+    block = lax.axis_index("tm")
+    kept = plan.inputs * plan.frames * plan.tiles
+    view = voltages.reshape(voltages.shape[0], 2, -1, LANES).transpose(0, 2, 1, 3).reshape(-1, LANES)
+    sent = lax.dynamic_slice_in_dim(view, (1 - block) * kept, kept, 0).astype(jnp.bfloat16)
+    recv = lax.ppermute(sent, "tm", [(0, 1), (1, 0)])
+    taps = (filter_taps / 64.0).reshape(plan.taps, -1, 1, LANES)
+    taps = jnp.broadcast_to(taps, (plan.taps, plan.tiles // 2, 2, LANES)).reshape(-1, LANES)
+    table = transform_table(plan)
+    where = jnp.stack([block.astype(jnp.int32), reference_channel[0]])
+    spectra = channelize(plan, where, view, recv, taps, table)
+    moved = lax.all_to_all(spectra, ("stn", "tm"), split_axis=0, concat_axis=0, tiled=True)
+    projection, power = subspace(plan, moved, basis_inputs)
+    power = power.reshape(plan.chans, plan.spectra)
+    subspace_power = lax.all_to_all(power, "tm", split_axis=1, concat_axis=0, tiled=True)
+    covariance = covariances(plan, moved)
+    return (covariance, projection, subspace_power)
+
+
+def on_device(voltages, filter_taps, reference_channel, basis_inputs):
+    plan = Plan(voltages, filter_taps)
+    body = functools.partial(packed_plan, plan) if plan.packed() else plain_plan
+    return body(voltages, filter_taps, reference_channel, basis_inputs)
+
+
 def solution(mesh):
     return jax.shard_map(
         on_device,

time: 582 us -> 111 us (0.19); the launches traced: 575 us -> 111 us
  other arithmetic: 212 us -> 2.99 us
  matrix products: 152 us -> 0 us
  local copies, waits for them, and re-layouts: 104 us -> 5.42 us
  blocking collectives: 70.4 us -> 0 us
  Pallas kernels: 0 us -> 46.8 us
  waiting for transfers between devices: 15.4 us -> 41.9 us
  between operations: 7.33 us -> 1.37 us
    dot_general x24 -> x0, matrix products: 152 us -> none  [the longest x2 22.7 us: block_sums(): jnp.einsum('itc,jtc->cij', part_real, part_imag, preferred_element_type=j...]
    pallas_call x0 -> x4, Pallas kernels: none -> 46.8 us  [the longest x1 21.1 us: channelize(): pl.pallas_call(functools.partial(channelize_kernel, plan, half), grid_spe...]
    add x2 -> x0, other arithmetic: 46.3 us -> none  [add_block(): return total + rounded]
    reduce_sum x15 -> x0, other arithmetic: 44.9 us -> none  [the longest x7 30.9 us: orthonormal(): inner_real = jnp.sum(q_real * vec_real + q_imag * vec_imag)]
    mul x2 -> x0, other arithmetic: 44 us -> none  [the longest x1 35 us: orthonormal(): basis_imag.append(vec_imag * inverse)]
    psum x1 -> x0, blocking collectives: 40 us -> none  [spread(): return lax.psum(jnp.where(mine, shard, jnp.zeros_like(shard)), axis)]
    while x1 -> x0, local copies, waits for them, and re-layouts: 31.9 us -> none  [blockwise_covariance(): return lax.fori_loop(0, blocks, add_block, start)]
    all_to_all x1 -> x0, blocking collectives: 30.4 us -> none  [on_device(): lax.all_to_all(spectra, 'stn', split_axis=2, concat_axis=0, tiled=True)]
  transfers between devices with their start and end apart: 3 -> 3, of which waited for: 2 -> 2; matrix products, arithmetic and copies ran while one was open for 13% -> 1% of each run, Pallas kernels for 0% -> 19%
where the time goes in v1:
time: 111 us
  Pallas kernels  46.8 us (42%)
  waiting for transfers between devices  41.9 us (38%)
  starting transfers between devices  12.4 us (11%)
  local copies, waits for them, and re-layouts  5.42 us (5%)
  other arithmetic  2.99 us (3%)
  between operations  1.37 us (1%)
    all_to_all x1, waiting for transfers between devices, packed_plan(): lax.all_to_all(spectra, ('stn', 'tm'), split_axis=0, concat_axis=0, tiled...  26.9 us
    pallas_call x1, Pallas kernels, channelize(): pl.pallas_call(functools.partial(channelize_kernel, plan, half), grid_spe...  21.1 us
    ppermute x1, waiting for transfers between devices, packed_plan(): recv = lax.ppermute(sent, 'tm', [(0, 1), (1, 0)])  15 us
    pallas_call x1, Pallas kernels, covariances(): pl.pallas_call(functools.partial(covariance_kernel, plan), grid=(plan.cha...  14.2 us
    pallas_call x1, Pallas kernels, transform_table(): pl.pallas_call(functools.partial(table_kernel, plan, rows), grid=(total /...  6.89 us
    all_to_all x1, starting transfers between devices, packed_plan(): lax.all_to_all(spectra, ('stn', 'tm'), split_axis=0, concat_axis=0, tiled...  6.1 us
    pallas_call x1, Pallas kernels, subspace(): pl.pallas_call(functools.partial(basis_kernel, plan, count), out_shape=(j...  4.62 us
    all_to_all x1, starting transfers between devices, packed_plan(): lax.all_to_all(power, 'tm', split_axis=1, concat_axis=0, tiled=True)  3.22 us
  transfers between devices with their start and end apart: 3, of which 2 were waited for; matrix products, arithmetic and copies ran while one was open for 1% of the time, Pallas kernels for 19%

profile of v1, /device:TPU:0, one launch (start us, length us, event | category | flops | bytes accessed | tf_op | source)
XLA Modules:
  0.0 110.8 jit_solution(7000636612838347876)
XLA Ops:
  0.6 0.0 copy-start.2
  0.6 1.7 %dynamic-slice_convert_fusion = bf16[4096,128]{1,0:T(8,128)(2,1)S(1)} fusion(s32[8192,128]{1,0:T(8,128)} %bitcast.18, s32[]{:T(128)S(6)} %select_n.3), kind=kLoop, calls=%fused_computation | loop fusion | flops 524288 | bytes 3145732 | tf_op jit(solution)/shard_map/convert_element_type | solution.py:529
  2.4 3.0 %collective-permute-start = (bf16[4096,128]{1,0:T(8,128)(2,1)S(1)}, bf16[4096,128]{1,0:T(8,128)(2,1)S(1)}, u32[]{:S(2)}, u32[]{:S(2)}) collective-permute-start(bf16[4096,128]{1,0:T(8,128)(2,1)S(1)} %dynamic-slice_convert_fusion), channel_id=1, source_target_pairs={{0,1},{1,0},{2,3},{3,2},{4,5},{5,4},{6,7},{7,6},{8,9},{9,8},{10,11... | collective-permute-start | bytes 3145736 | tf_op jit(solution)/shard_map/ppermute | solution.py:530
  5.4 6.9 %table.1.table_hbm = bf16[1024,2048]{1,0:T(8,128)(2,1)} custom-call(), custom_call_target="tpu_custom_call" | custom-call | tf_op jit(solution)/shard_map/table/pallas_call | solution.py:244
  13.0 0.0 copy-done.2
  13.0 0.6 pad_add_fusion.where_ref
  13.6 15.0 %collective-permute-done.recv_ref = bf16[4096,128]{1,0:T(8,128)(2,1)S(1)} collective-permute-done((bf16[4096,128]{1,0:T(8,128)(2,1)S(1)}, bf16[4096,128]{1,0:T(8,128)(2,1)S(1)}, u32[]{:S(2)}, u32[]{:S(2)}) %collective-permute-start) | collective-permute-done | bytes 1048608 | tf_op jit(solution)/shard_map/ppermute | solution.py:530
  28.6 0.0 copy-start.1
  28.6 0.8 broadcast_in_dim.8
  29.4 0.2 copy-done.1
  29.6 0.0 copy-start.3
  29.6 21.1 %channelize.1 = bf16[32,136,128]{2,1,0:T(8,128)(2,1)} custom-call(s32[2]{0:T(128)} %pad_add_fusion.where_ref, s32[8192,128]{1,0:T(8,128)} %bitcast.19, bf16[4096,128]{1,0:T(8,128)(2,1)} %copy-done.1, f32[256,128]{1,0:T(8,128)} %bitcast.20, bf16[1024,2048]{1,0:T(8,128)(2,1)} %table.1.table_hbm), custom_call_target="tpu_custom_call" | custom-call | tf_op jit(solution)/shard_map/channelize/pallas_call | solution.py:361
  50.7 6.1 %all-to-all-start = ((bf16[32,136,128]{2,1,0:T(8,128)(2,1)}), bf16[32,136,128]{2,1,0:T(8,128)(2,1)S(1)}, u32[]{:S(2)}, u32[]{:S(2)}) async-start(bf16[32,136,128]{2,1,0:T(8,128)(2,1)} %channelize.1), calls=%async_computation | async-start | bytes 2228224 | tf_op jit(solution)/shard_map/all_to_all | solution.py:536
  56.8 0.0 copy-done.3
  56.8 0.7 copy.11.picks_ref
  57.5 26.9 %all-to-all-done.real_ref.imag_ref.recv_ref = bf16[32,136,128]{2,1,0:T(8,128)(2,1)S(1)} async-done(((bf16[32,136,128]{2,1,0:T(8,128)(2,1)}), bf16[32,136,128]{2,1,0:T(8,128)(2,1)S(1)}, u32[]{:S(2)}, u32[]{:S(2)}) %all-to-all-start) | async-done | bytes 1114144 | tf_op jit(solution)/shard_map/all_to_all | solution.py:536
  84.4 0.0 copy-start
  84.4 1.0 copy-done
  85.4 4.6 %subspace.1 = (f32[16,128]{1,0:T(8,128)}, f32[4,128]{1,0:T(4,128)}) custom-call(bf16[32,136,128]{2,1,0:T(8,128)(2,1)} %copy-done, s32[8,1]{1,0:T(8,128)} %copy.11.picks_ref), custom_call_target="tpu_custom_call" | custom-call | tf_op jit(solution)/shard_map/subspace/pallas_call | solution.py:484
  90.0 0.8 all_to_all.18
  90.8 0.7 reshape.29
  91.5 3.2 %all-to-all-start.1 = ((f32[2,1,256]{2,1,0:T(1,128)}), f32[2,1,256]{2,1,0:T(1,128)S(1)}, u32[]{:S(2)}, u32[]{:S(2)}) async-start(f32[2,1,256]{2,1,0:T(1,128)} %reshape.29), calls=%async_computation.1 | async-start | bytes 4096 | tf_op jit(solution)/shard_map/all_to_all | solution.py:539
  94.7 14.2 %covariance.1 = bf16[16,512,1024]{2,1,0:T(8,128)(2,1)} custom-call(bf16[32,136,128]{2,1,0:T(8,128)(2,1)} %copy-done, bf16[32,136,128]{2,1,0:T(8,128)(2,1)} %copy-done), custom_call_target="tpu_custom_call" | custom-call | tf_op jit(solution)/shard_map/covariance/pallas_call | solution.py:512
  108.9 0.0 all-to-all-done.1
  108.9 0.5 broadcast.1
  109.4 0.7 reduce
  110.1 0.1 reshape.30
  110.1 0.7 copy.13
  (3 shorter events, 0.0 us)
Async XLA Ops:
  0.6 12.3 %copy-start.2 = (f32[16,1024]{1,0:T(8,128)S(1)}, f32[16,1024]{1,0:T(8,128)}, u32[]{:S(2)}) copy-start(f32[16,1024]{1,0:T(8,128)} %param.5) | copy-start | bytes 196612
  2.4 26.2 %collective-permute-start = (bf16[4096,128]{1,0:T(8,128)(2,1)S(1)}, bf16[4096,128]{1,0:T(8,128)(2,1)S(1)}, u32[]{:S(2)}, u32[]{:S(2)}) collective-permute-start(bf16[4096,128]{1,0:T(8,128)(2,1)S(1)} %dynamic-slice_convert_fusion), channel_id=1, source_target_pairs={{0,1},{1,0},{2,3},{3,2},{4,5},{5,4},{6,7},{7,6},{8,9},{9,8},{10,11... | collective-permute-start | bytes 3145736 | tf_op jit(solution)/shard_map/ppermute | solution.py:530
  28.6 1.0 copy-start.1
  29.6 27.2 %copy-start.3 = (s32[8]{0:T(128)S(1)}, s32[8]{0:T(128)}, u32[]{:S(2)}) copy-start(s32[8]{0:T(128)} %param.7) | copy-start | bytes 100
  50.7 33.7 %all-to-all-start = ((bf16[32,136,128]{2,1,0:T(8,128)(2,1)}), bf16[32,136,128]{2,1,0:T(8,128)(2,1)S(1)}, u32[]{:S(2)}, u32[]{:S(2)}) async-start(bf16[32,136,128]{2,1,0:T(8,128)(2,1)} %channelize.1), calls=%async_computation | async-start | bytes 2228224 | tf_op jit(solution)/shard_map/all_to_all | solution.py:536
  84.4 1.0 copy-start
  91.5 17.4 %all-to-all-start.1 = ((f32[2,1,256]{2,1,0:T(1,128)}), f32[2,1,256]{2,1,0:T(1,128)S(1)}, u32[]{:S(2)}, u32[]{:S(2)}) async-start(f32[2,1,256]{2,1,0:T(1,128)} %reshape.29), calls=%async_computation.1 | async-start | bytes 4096 | tf_op jit(solution)/shard_map/all_to_all | solution.py:539

commit v2 on v1

--- a/solution.py
+++ b/solution.py
@@ -195,8 +195,6 @@
         self.tiles = 2 * self.nfft // LANES
         self.group = LANES // self.spectra
         self.quads = self.chans // max(self.group, 1)
-        self.chunk = 2 * self.quads * self.inputs
-        self.extra = self.inputs // 2
 
     def packed(self):
         return (
@@ -209,7 +207,7 @@
         )
 
 
-def table_kernel(plan, rows, out_ref):
+def table_kernel(plan, rows, taps_ref, out_ref, lanes_ref):
     shape = (rows, LANES)
     row = lax.broadcasted_iota(jnp.int32, shape, 0) + pl.program_id(0) * rows
     lane = lax.broadcasted_iota(jnp.int32, shape, 1)
@@ -228,6 +226,20 @@
     turn = lax.rem(channel * LANES, plan.nfft).astype(jnp.float32) * unit
     turn_cos = jnp.cos(turn)
     turn_sin = jnp.sin(turn)
+    spot = lax.div(lax.broadcasted_iota(jnp.int32, (SUB, LANES), 0), 2)
+
+    @pl.when(pl.program_id(0) == 0)
+    def _():
+        for k in range(plan.taps):
+            for sub in range(ROWS // SUB):
+                made = jnp.zeros((SUB, LANES), jnp.float32)
+                for n in range(SUB // 2):
+                    first = (sub * SUB // 2 + n) * LANES
+                    line = taps_ref[k : k + 1, first : first + LANES] * (1.0 / 64.0)
+                    made = jnp.where(spot == n, jnp.broadcast_to(line, (SUB, LANES)), made)
+                at = k * ROWS + sub * SUB
+                lanes_ref[at : at + SUB, :] = made
+
     for tile in range(plan.nfft // LANES):
         first = 2 * tile * LANES
         out_ref[:, first : first + LANES] = cosine.astype(jnp.bfloat16)
@@ -238,16 +250,23 @@
         )
 
 
-def transform_table(plan):
+def transform_table(plan, filter_taps):
     rows = 128
     total = plan.nfft
     return pl.pallas_call(
         functools.partial(table_kernel, plan, rows),
         grid=(total // rows,),
-        out_specs=pl.BlockSpec((rows, 2 * plan.nfft), lambda r: (r, 0)),
-        out_shape=jax.ShapeDtypeStruct((total, 2 * plan.nfft), jnp.bfloat16),
+        in_specs=[pl.BlockSpec(filter_taps.shape, lambda r: (0, 0))],
+        out_specs=[
+            pl.BlockSpec((rows, 2 * plan.nfft), lambda r: (r, 0)),
+            pl.BlockSpec((plan.taps * ROWS, LANES), lambda r: (0, 0)),
+        ],
+        out_shape=[
+            jax.ShapeDtypeStruct((total, 2 * plan.nfft), jnp.bfloat16),
+            jax.ShapeDtypeStruct((plan.taps * ROWS, LANES), jnp.float32),
+        ],
         name="table",
-    )()
+    )(filter_taps)
 
 
 def lane_iota(rows):
@@ -270,26 +289,31 @@
     return out
 
 
-def channelize_kernel(
-    plan, half, where_ref, own_ref, recv_ref, taps_ref, table_hbm, out_ref, table, sig, filt, low, prod, spread_f32, sem
-):
-    step = pl.program_id(0)
-    block = where_ref[0]
-    copy = pltpu.make_async_copy(table_hbm, table, sem)
-
-    @pl.when(step == 0)
-    def _():
-        copy.start()
-
-    frames, spectra, taps = plan.frames, plan.spectra, plan.taps
+def channelize_kernel(plan, part, where_ref, own_hbm, recv_ref, taps_ref, table_hbm, *refs):
+    first_ref = refs[0] if part else None
+    outs = refs[1:2] if part else refs[0:2]
+    table, own, sig, filt, low, prod, ref_f32, sems = refs[2:]
+    half, frames, spectra, taps = plan.inputs // 2, plan.frames, plan.spectra, plan.taps
     span = frames * ROWS
+    block = lax.axis_index("tm")
+    pieces = 4
+    each = half // pieces
+    start = pl.multiple_of((block * 2 + part) * (half * span), half * span)
+    loads = []
+    for n in range(pieces):
+        rows = each * span
+        source = own_hbm.at[pl.ds(start + n * rows, rows), :]
+        loads.append(pltpu.make_async_copy(source, own.at[pl.ds(n * rows, rows), :], sems.at[n]))
+    loads.append(pltpu.make_async_copy(table_hbm, table, sems.at[pieces]))
+    for load in loads:
+        load.start()
 
     def one_input(i, carry):
         own_at = pl.multiple_of(block * span, span)
         recv_at = pl.multiple_of((1 - block) * span, span)
-        start = pl.multiple_of(i * span, span)
-        sig[pl.ds(own_at, span), :] = own_ref[pl.ds(start, span), :].astype(jnp.float32)
-        sig[pl.ds(recv_at, span), :] = recv_ref[pl.ds(start, span), :].astype(jnp.float32)
+        at = pl.multiple_of(i * span, span)
+        sig[pl.ds(own_at, span), :] = own[pl.ds(at, span), :].astype(jnp.float32)
+        sig[pl.ds(recv_at, span), :] = recv_ref[pl.ds(at, span), :].astype(jnp.float32)
         base = pl.multiple_of(i * (spectra * ROWS), spectra * ROWS)
         for sub in range(ROWS // SUB):
             tap = [taps_ref[k * ROWS + sub * SUB : k * ROWS + (sub + 1) * SUB, :] for k in range(taps)]
@@ -302,95 +326,84 @@
                 filt[pl.ds(base + t * ROWS + sub * SUB, SUB), :] = acc
         return carry
 
-    lax.fori_loop(0, half, one_input, 0)
+    for n in range(pieces):
+        loads[n].wait()
+        lax.fori_loop(n * each, (n + 1) * each, one_input, 0)
     for tile in range(plan.tiles):
         picked = filt[pl.ds(tile, half * spectra, stride=ROWS), :]
         low[:, tile * LANES : (tile + 1) * LANES] = picked.astype(jnp.bfloat16)
-
-    @pl.when(step == 0)
-    def _():
-        copy.wait()
-
+    loads[pieces].wait()
     prod[...] = nt_dot(table[...], low[...])
     per_dest = plan.group * SUB
 
+    def regrouped(d, cols):
+        rows = pl.multiple_of(d * per_dest, per_dest)
+        lanes = slice(cols * LANES, (cols + 1) * LANES)
+        return regroup([prod[pl.ds(rows + c * SUB, SUB), lanes] for c in range(plan.group)])
+
+    out_ref = outs[0]
+
     def one_dest(d, carry):
-        rows = pl.multiple_of(d * per_dest, per_dest)
-        for part in range(half // plan.group):
-            cols = slice(part * LANES, (part + 1) * LANES)
-            moved = regroup([prod[pl.ds(rows + c * SUB, SUB), cols] for c in range(plan.group)])
-            for b in range(plan.group):
-                at = d * (SUB * ROWS) + step * half + part * plan.group + b
-                spread_f32[pl.ds(at, SUB, stride=ROWS), :] = moved[b]
+        for cols in range(half // plan.group):
+            moved = regrouped(d, cols)
+            for b in range(0, plan.group, 2):
+                at = (cols * plan.group + b) * SUB
+                pair = jnp.concatenate(moved[b : b + 2], axis=0)
+                out_ref[d, at : at + 2 * SUB, :] = pair.astype(jnp.bfloat16)
         return carry
 
-    lax.fori_loop(0, plan.devices, one_dest, 0)
-
-    @pl.when(step == pl.num_programs(0) - 1)
-    def _():
-        channel = where_ref[1]
-        owner = lax.div(channel, plan.chans)
-        local = lax.rem(channel, plan.chans)
-        quad = lax.div(local, plan.group)
-        member = lax.rem(local, plan.group)
-        lane = lane_iota(ROWS)
-        tiles = []
-        for part in range(2):
-            at = pl.multiple_of((owner * SUB + part * plan.quads + quad) * ROWS, ROWS)
-            tiles.append(spread_f32[pl.ds(at, ROWS), :])
-        shift = LANES - member * plan.spectra
-        real = pltpu.roll(tiles[0], lax.rem(shift, LANES), 1)
-        imag = pltpu.roll(tiles[1], lax.rem(shift + plan.spectra, LANES), 1)
-        both = jnp.where(lane < plan.spectra, real, imag)
-        folded = jnp.where(lane_iota(SUB) < 64, both[:SUB], pltpu.roll(both[SUB:], 64, 1))
-        folded = folded.astype(jnp.bfloat16)
-
-        def finish(d, carry):
-            at = pl.multiple_of(d * plan.chunk, plan.chunk)
-            out_ref[d, : plan.chunk, :] = spread_f32[pl.ds(at, plan.chunk), :].astype(jnp.bfloat16)
-            out_ref[d, plan.chunk :, :] = folded
-            return carry
-
-        lax.fori_loop(0, plan.devices, finish, 0)
-
-
-def channelize(plan, where, own, recv, taps, table):
+    lax.fori_loop(0, plan.devices, one_dest, 0, unroll=8)
+    channel = where_ref[0]
+    owner = lax.div(channel, plan.chans)
+    local = lax.rem(channel, plan.chans)
+    quad = lax.div(local, plan.group)
+    member = lax.rem(local, plan.group)
+    for cols in range(half // plan.group):
+        moved = regrouped(owner, cols)
+        for b in range(plan.group):
+            at = (cols * plan.group + b) * SUB
+            ref_f32[at : at + SUB, :] = moved[b]
+    lane = lane_iota(SUB)
+    shift = LANES - member * spectra
+    real = ref_f32[pl.ds(quad, half, stride=SUB), :]
+    imag = ref_f32[pl.ds(plan.quads + quad, half, stride=SUB), :]
+    real = pltpu.roll(real, lax.rem(shift, LANES), 1)
+    imag = pltpu.roll(imag, lax.rem(shift + spectra, LANES), 1)
+    both = jnp.where(lane < spectra, real, imag)
+    if part == 0:
+        outs[1][...] = both
+        return
+    folded = jnp.where(lane < 2 * spectra, first_ref[...], pltpu.roll(both, 2 * spectra, 1))
+    folded = folded.astype(jnp.bfloat16)
+    for d in range(plan.devices):
+        out_ref[d, half * SUB :, :] = folded
+
+
+def channelize(plan, part, where, own, recv, taps, table, first):
     half = plan.inputs // 2
     rows = half * plan.frames * ROWS
-    out = (plan.devices, plan.chunk + plan.extra, LANES)
+    whole = pl.BlockSpec(memory_space=pltpu.VMEM)
+    hbm = pl.BlockSpec(memory_space=pl.ANY)
+    chunk = half * SUB
+    out_shape = [jax.ShapeDtypeStruct((plan.devices, chunk + part * SUB, LANES), jnp.bfloat16)]
+    if part == 0:
+        out_shape.append(jax.ShapeDtypeStruct((half, LANES), jnp.float32))
     return pl.pallas_call(
-        functools.partial(channelize_kernel, plan, half),
-        grid_spec=pltpu.PrefetchScalarGridSpec(
-            num_scalar_prefetch=1,
-            grid=(2,),
-            in_specs=[
-                pl.BlockSpec((rows, LANES), lambda g, w: (w[0] * 2 + g, 0)),
-                pl.BlockSpec((rows, LANES), lambda g, w: (g, 0)),
-                pl.BlockSpec(taps.shape, lambda g, w: (0, 0)),
-                pl.BlockSpec(memory_space=pl.ANY),
-            ],
-            out_specs=pl.BlockSpec(out, lambda g, w: (0, 0, 0)),
-            scratch_shapes=[
-                pltpu.VMEM(table.shape, jnp.bfloat16),
-                pltpu.VMEM((plan.spectra * ROWS, LANES), jnp.float32),
-                pltpu.VMEM((half * plan.spectra * ROWS, LANES), jnp.float32),
-                pltpu.VMEM((half * plan.spectra, 2 * plan.nfft), jnp.bfloat16),
-                pltpu.VMEM((plan.nfft, half * plan.spectra), jnp.float32),
-                pltpu.VMEM((plan.devices * plan.chunk, LANES), jnp.float32),
-                pltpu.SemaphoreType.DMA(()),
-            ],
-        ),
-        out_shape=jax.ShapeDtypeStruct(out, jnp.bfloat16),
-        name="channelize",
-    )(where, own, recv, taps, table)
-
-
-def pair_of(recv_ref, plan, quad):
-    shape = (plan.inputs_all, LANES)
-    real = recv_ref[:, quad * ROWS : (quad + 1) * ROWS, :].reshape(shape)
-    at = (plan.quads + quad) * ROWS
-    imag = recv_ref[:, at : at + ROWS, :].reshape(shape)
-    return real, imag
+        functools.partial(channelize_kernel, plan, part),
+        in_specs=[pl.BlockSpec(memory_space=pltpu.SMEM), hbm, whole, whole, hbm] + [whole] * part,
+        out_specs=[whole] * len(out_shape),
+        scratch_shapes=[
+            pltpu.VMEM(table.shape, jnp.bfloat16),
+            pltpu.VMEM((rows, LANES), jnp.int32),
+            pltpu.VMEM((plan.spectra * ROWS, LANES), jnp.float32),
+            pltpu.VMEM((half * plan.spectra * ROWS, LANES), jnp.float32),
+            pltpu.VMEM((half * plan.spectra, 2 * plan.nfft), jnp.bfloat16),
+            pltpu.VMEM((plan.nfft, half * plan.spectra), jnp.float32),
+            pltpu.VMEM((half * SUB, LANES), jnp.float32),
+            pltpu.SemaphoreType.DMA((5,)),
+        ],
+        out_shape=out_shape,
+    )(where, own, recv, taps, table, *([first] * part))
 
 
 def inverse_root(value):
@@ -398,10 +411,22 @@
     return y * (1.5 - 0.5 * value * y * y)
 
 
-def basis_kernel(plan, count, recv_ref, picks_ref, proj_ref, power_ref):
+def basis_kernel(
+    plan, count, one_ref, two_ref, picks_ref, x_ref, proj_ref, keep_ref, send_ref, one, two, spot_power, turned_power
+):
     highest = lax.Precision.HIGHEST
     span = plan.spectra
-    folded = recv_ref[:, plan.chunk :, :].astype(jnp.float32)
+    half = plan.inputs // 2
+    chunk = half * SUB
+    one[...] = one_ref[...].reshape(one.shape).astype(jnp.float32)
+    two[...] = two_ref[:, :chunk, :].reshape(two.shape).astype(jnp.float32)
+    for n in range(SUB):
+        parts = [
+            h[pl.ds(n, plan.devices * half, stride=SUB), :].reshape(plan.devices, half, LANES)
+            for h in (one, two)
+        ]
+        x_ref[n] = jnp.concatenate(parts, axis=1).reshape(plan.inputs_all, LANES).astype(jnp.bfloat16)
+    folded = two_ref[:, chunk:, :].astype(jnp.float32)
     turned = pltpu.roll(folded.reshape(-1, LANES), 64, 1).reshape(folded.shape)
     ref = jnp.concatenate([folded, turned], axis=1).reshape(plan.inputs_all, LANES)
     ref = ref.astype(jnp.bfloat16)
@@ -457,14 +482,18 @@
     wide = lax.broadcasted_iota(jnp.int32, (members, 2 * size), 1)
     tall = lax.broadcasted_iota(jnp.int32, (members, 2 * size), 0)
     keep = lax.rem(lax.div(wide, count), count) == lax.rem(tall, count)
+    own_lanes = lax.broadcasted_iota(jnp.int32, (plan.group, LANES), 0) == lax.div(lane_iota(plan.group), span)
     for quad in range(plan.quads):
-        xr, xi = pair_of(recv_ref, plan, quad)
+        xr = x_ref[quad]
+        xi = x_ref[plan.quads + quad]
         sr = jnp.dot(stack, xr, preferred_element_type=jnp.float32)
         si = jnp.dot(stack, xi, preferred_element_type=jnp.float32)
         piece = lambda s, n: s[n * count : (n + 1) * count]
         low_r = piece(sr, 0) + piece(si, 1)
         low_i = piece(si, 0) - piece(sr, 1)
-        power_ref[quad : quad + 1, :] = jnp.sum(low_r * low_r + low_i * low_i, axis=0, keepdims=True)
+        power = jnp.sum(low_r * low_r + low_i * low_i, axis=0, keepdims=True)
+        power = jnp.where(own_lanes, jnp.broadcast_to(power, own_lanes.shape), 0.0)
+        spot_power[quad * plan.group : (quad + 1) * plan.group, :] = power
         yr = low_r + ((piece(sr, 2) + piece(si, 3)) + (piece(sr, 4) + piece(si, 5)))
         yi = low_i + ((piece(si, 2) - piece(sr, 3)) + (piece(si, 4) - piece(sr, 5)))
         tiled_r = jnp.where(mine, jnp.concatenate([yr] * plan.group, axis=0), 0.0)
@@ -477,74 +506,106 @@
         placed = jnp.dot(gram_r, put_r, precision=highest) + jnp.dot(gram_i, put_i, precision=highest)
         placed = jnp.where(keep, placed, 0.0).reshape(plan.group, count, 2 * size)
         proj_ref[quad * plan.group : (quad + 1) * plan.group, :] = jnp.sum(placed, axis=1)
-
-
-def subspace(plan, recv, basis_inputs):
+    time = lax.broadcasted_iota(jnp.int32, (span, LANES), 0)
+    same = jnp.where(lax.rem(lane_iota(span), span) == time, 1.0, 0.0)
+    turned_power[...] = nt_dot(same, spot_power[...], highest)
+    block = lax.axis_index("tm")
+    keep_ref[...] = turned_power[pl.ds(pl.multiple_of(block * plan.frames, plan.frames), plan.frames), :]
+    send_ref[...] = turned_power[pl.ds(pl.multiple_of((1 - block) * plan.frames, plan.frames), plan.frames), :]
+
+
+def subspace(plan, one, two, basis_inputs):
     count = basis_inputs.shape[0]
+    whole = pl.BlockSpec(memory_space=pltpu.VMEM)
+    unpacked = pltpu.VMEM((plan.devices * plan.inputs // 2 * SUB, LANES), jnp.float32)
+    power = jax.ShapeDtypeStruct((plan.frames, plan.chans), jnp.float32)
     return pl.pallas_call(
         functools.partial(basis_kernel, plan, count),
+        in_specs=[whole, whole, whole],
+        out_specs=[whole] * 4,
         out_shape=(
+            pltpu.VMEM((SUB, plan.inputs_all, LANES), jnp.bfloat16),
             jax.ShapeDtypeStruct((plan.chans, 2 * count * count), jnp.float32),
-            jax.ShapeDtypeStruct((plan.quads, LANES), jnp.float32),
+            power,
+            power,
         ),
+        scratch_shapes=[
+            unpacked,
+            unpacked,
+            pltpu.VMEM((plan.chans, LANES), jnp.float32),
+            pltpu.VMEM((plan.spectra, plan.chans), jnp.float32),
+        ],
         name="subspace",
-    )(recv, basis_inputs.reshape(count, 1))
-
-
-def covariance_kernel(plan, real_ref, imag_ref, out_ref):
-    member = lax.rem(pl.program_id(0), plan.group)
-    shape = (plan.inputs_all, LANES)
-    real = real_ref[...].reshape(shape)
-    imag = imag_ref[...].reshape(shape)
-    inside = lax.div(lax.broadcasted_iota(jnp.int32, (1, LANES), 1), plan.spectra) == member
-    mask = jnp.where(inside, 1.0 / plan.spectra, 0.0).astype(jnp.bfloat16)
-    left_r = real * mask
-    left_i = imag * mask
+    )(one, two, basis_inputs.reshape(count, 1))
+
+
+PER_STEP = 2
+
+
+def covariance_kernel(plan, x_ref, out_ref):
+    step = pl.program_id(0)
+    quad = lax.div(step * PER_STEP, plan.group)
+    real = x_ref[quad]
+    imag = x_ref[plan.quads + quad]
     right = jnp.concatenate([real, imag], axis=1)
     total = plan.inputs_all
-    out_ref[0, :, :total] = nt_dot(jnp.concatenate([left_r, left_i], axis=1), right).astype(jnp.bfloat16)
-    out_ref[0, :, total:] = nt_dot(jnp.concatenate([left_i, -left_r], axis=1), right).astype(jnp.bfloat16)
-
-
-def covariances(plan, recv):
+    for n in range(PER_STEP):
+        member = lax.rem(step * PER_STEP, plan.group) + n
+        inside = lax.div(lax.broadcasted_iota(jnp.int32, (1, LANES), 1), plan.spectra) == member
+        mask = jnp.where(inside, 1.0 / plan.spectra, 0.0).astype(jnp.bfloat16)
+        left_r = real * mask
+        left_i = imag * mask
+        out_ref[n, :, :total] = nt_dot(jnp.concatenate([left_r, left_i], axis=1), right).astype(jnp.bfloat16)
+        out_ref[n, :, total:] = nt_dot(jnp.concatenate([left_i, -left_r], axis=1), right).astype(jnp.bfloat16)
+
+
+def covariances(plan, x):
     out = (plan.chans, plan.inputs_all, 2 * plan.inputs_all)
-    block = (plan.devices, ROWS, LANES)
     return pl.pallas_call(
         functools.partial(covariance_kernel, plan),
-        grid=(plan.chans,),
-        in_specs=[
-            pl.BlockSpec(block, lambda c: (0, c // plan.group, 0)),
-            pl.BlockSpec(block, lambda c: (0, plan.quads + c // plan.group, 0)),
-        ],
-        out_specs=pl.BlockSpec((1, *out[1:]), lambda c: (c, 0, 0)),
+        grid=(plan.chans // PER_STEP,),
+        in_specs=[pl.BlockSpec(memory_space=pltpu.VMEM)],
+        out_specs=pl.BlockSpec((PER_STEP, *out[1:]), lambda c: (c, 0, 0)),
         out_shape=jax.ShapeDtypeStruct(out, jnp.bfloat16),
         name="covariance",
-    )(recv, recv)
+    )(x)
+
+
+def on_chip(array):
+    return pltpu.with_memory_space_constraint(array, pltpu.VMEM)
 
 
 def packed_plan(plan, voltages, filter_taps, reference_channel, basis_inputs):
     block = lax.axis_index("tm")
-    kept = plan.inputs * plan.frames * plan.tiles
+    kept = plan.inputs * plan.frames * plan.tiles // 2
     view = voltages.reshape(voltages.shape[0], 2, -1, LANES).transpose(0, 2, 1, 3).reshape(-1, LANES)
-    sent = lax.dynamic_slice_in_dim(view, (1 - block) * kept, kept, 0).astype(jnp.bfloat16)
-    recv = lax.ppermute(sent, "tm", [(0, 1), (1, 0)])
-    taps = (filter_taps / 64.0).reshape(plan.taps, -1, 1, LANES)
-    taps = jnp.broadcast_to(taps, (plan.taps, plan.tiles // 2, 2, LANES)).reshape(-1, LANES)
-    table = transform_table(plan)
-    where = jnp.stack([block.astype(jnp.int32), reference_channel[0]])
-    spectra = channelize(plan, where, view, recv, taps, table)
-    moved = lax.all_to_all(spectra, ("stn", "tm"), split_axis=0, concat_axis=0, tiled=True)
-    projection, power = subspace(plan, moved, basis_inputs)
-    power = power.reshape(plan.chans, plan.spectra)
-    subspace_power = lax.all_to_all(power, "tm", split_axis=1, concat_axis=0, tiled=True)
-    covariance = covariances(plan, moved)
-    return (covariance, projection, subspace_power)
+    swap = [(0, 1), (1, 0)]
+    recv = []
+    for part in range(2):
+        start = ((1 - block) * 2 + part) * kept
+        sent = lax.dynamic_slice_in_dim(view, start, kept, 0).astype(jnp.bfloat16)
+        recv.append(lax.ppermute(sent, "tm", swap))
+    table, taps = transform_table(plan, filter_taps)
+    both = ("stn", "tm")
+    recv = [on_chip(r) for r in recv]
+    sent, first = channelize(plan, 0, reference_channel, view, recv[0], taps, table, None)
+    one = lax.all_to_all(sent, both, split_axis=0, concat_axis=0, tiled=True)
+    (sent,) = channelize(plan, 1, reference_channel, view, recv[1], taps, table, first)
+    two = lax.all_to_all(sent, both, split_axis=0, concat_axis=0, tiled=True)
+    x, projection, keep, send = subspace(plan, on_chip(one), on_chip(two), basis_inputs)
+    other = lax.ppermute(send, "tm", swap)
+    covariance = covariances(plan, on_chip(x))
+    early = jnp.concatenate([keep, other], axis=1)
+    late = jnp.concatenate([other, keep], axis=1)
+    power = jnp.where(block == 0, early, late)
+    return (covariance, projection, power.T)
 
 
 def on_device(voltages, filter_taps, reference_channel, basis_inputs):
     plan = Plan(voltages, filter_taps)
-    body = functools.partial(packed_plan, plan) if plan.packed() else plain_plan
-    return body(voltages, filter_taps, reference_channel, basis_inputs)
+    if not plan.packed():
+        return plain_plan(voltages, filter_taps, reference_channel, basis_inputs)
+    return packed_plan(plan, voltages, filter_taps, reference_channel, basis_inputs)
 
 
 def solution(mesh):

time: 111 us -> 95.5 us (0.86)
  Pallas kernels: 46.8 us -> 36.4 us
  waiting for transfers between devices: 41.9 us -> 36.9 us
  starting transfers between devices: 12.4 us -> 17.4 us
  local copies, waits for them, and re-layouts: 5.42 us -> 0.68 us
    all_to_all x2, waiting for transfers between devices: 26.9 us -> 15.7 us  [the longest x1 15.7 us: packed_plan(): two = lax.all_to_all(sent, both, split_axis=0, concat_axis=0, tiled=True)]
    pallas_call x2 -> x3, Pallas kernels: 25.7 us -> 19.5 us  [the longest x2 15.2 us: channelize(): pl.pallas_call(functools.partial(channelize_kernel, plan, part), in_specs...]
    ppermute x1 -> x3, waiting for transfers between devices: 15 us -> 21.2 us  [the longest x2 21.2 us: packed_plan(): recv.append(lax.ppermute(sent, 'tm', swap))]
    pallas_call x1, Pallas kernels: 14.2 us -> 9.03 us  [covariances(): pl.pallas_call(functools.partial(covariance_kernel, plan), grid=(plan.cha...]
    ppermute x1 -> x3, starting transfers between devices: 3.03 us -> 6.63 us  [the longest x2 4.86 us: packed_plan(): recv.append(lax.ppermute(sent, 'tm', swap))]
    unnamed x12 -> x4, local copies, waits for them, and re-layouts: 2.68 us -> 0.01 us
    all_to_all x2, starting transfers between devices: 9.32 us -> 10.8 us  [the longest x1 6.11 us: packed_plan(): one = lax.all_to_all(sent, both, split_axis=0, concat_axis=0, tiled=True)]
    all_to_all x3 -> x0, local copies, waits for them, and re-layouts: 1.28 us -> none  [packed_plan(): lax.all_to_all(power, 'tm', split_axis=1, concat_axis=0, tiled=True)]
  transfers between devices with their start and end apart: 3 -> 5, of which waited for: 2 -> 3; matrix products, arithmetic and copies ran while one was open for 1% -> 1% of each run, Pallas kernels for 19% -> 26%
where the time goes in v2:
time: 95.5 us; the launch traced here: 95.1 us
  waiting for transfers between devices  36.9 us (39%)
  Pallas kernels  36.4 us (38%)
  starting transfers between devices  17.4 us (18%)
  other arithmetic  2.36 us (2%)
  between operations  1.35 us (1%)
    ppermute x2, waiting for transfers between devices, packed_plan(): recv.append(lax.ppermute(sent, 'tm', swap))  21.2 us
    all_to_all x1, waiting for transfers between devices, packed_plan(): two = lax.all_to_all(sent, both, split_axis=0, concat_axis=0, tiled=True)  15.7 us
    pallas_call x2, Pallas kernels, channelize(): pl.pallas_call(functools.partial(channelize_kernel, plan, part), in_specs...  15.2 us
    pallas_call x1, Pallas kernels, covariances(): pl.pallas_call(functools.partial(covariance_kernel, plan), grid=(plan.cha...  9.03 us
    pallas_call x1, Pallas kernels, transform_table(): pl.pallas_call(functools.partial(table_kernel, plan, rows), grid=(total /...  7.88 us
    all_to_all x1, starting transfers between devices, packed_plan(): one = lax.all_to_all(sent, both, split_axis=0, concat_axis=0, tiled=True)  6.11 us
    ppermute x2, starting transfers between devices, packed_plan(): recv.append(lax.ppermute(sent, 'tm', swap))  4.86 us
    all_to_all x1, starting transfers between devices, packed_plan(): two = lax.all_to_all(sent, both, split_axis=0, concat_axis=0, tiled=True)  4.65 us
  transfers between devices with their start and end apart: 5, of which 3 were waited for; matrix products, arithmetic and copies ran while one was open for 1% of the time, Pallas kernels for 26%

profile of v2, /device:TPU:0, one launch (start us, length us, event | category | flops | bytes accessed | tf_op | source)
XLA Modules:
  0.0 95.1 jit_solution(14219035577268737931)
XLA Ops:
  0.6 1.7 %dynamic-slice_convert_fusion = (bf16[2048,128]{1,0:T(8,128)(2,1)S(1)}, bf16[2048,128]{1,0:T(8,128)(2,1)S(1)}) fusion(s32[8192,128]{1,0:T(8,128)} %bitcast.8, s32[]{:T(128)S(6)} %select_n.15, s32[]{:T(128)S(6)} %select_n.14), kind=kLoop, calls=%fused_computation | loop fusion | flops 524288 | bytes 3145736 | tf_op jit(solution)/shard_map/convert_element_type | solution.py:586
  2.3 3.0 %collective-permute-start = (bf16[2048,128]{1,0:T(8,128)(2,1)S(1)}, bf16[2048,128]{1,0:T(8,128)(2,1)S(1)}, u32[]{:S(2)}, u32[]{:S(2)}) collective-permute-start(bf16[2048,128]{1,0:T(8,128)(2,1)S(1)} %get-tuple-element.20), channel_id=1, source_target_pairs={{0,1},{1,0},{2,3},{3,2},{4,5},{5,4},{6,7},{7,6},{8,9},{9,8},{10,11... | collective-permute-start | bytes 1572872 | tf_op jit(solution)/shard_map/ppermute | solution.py:587
  6.0 7.9 %table.1 = (bf16[1024,2048]{1,0:T(8,128)(2,1)}, f32[256,128]{1,0:T(8,128)}) custom-call(f32[16,1024]{1,0:T(8,128)} %taps_ref.1), custom_call_target="tpu_custom_call" | custom-call | tf_op jit(solution)/shard_map/table/pallas_call | solution.py:256
  13.9 3.4 %collective-permute-done.recv_ref = bf16[2048,128]{1,0:T(8,128)(2,1)S(1)} collective-permute-done((bf16[2048,128]{1,0:T(8,128)(2,1)S(1)}, bf16[2048,128]{1,0:T(8,128)(2,1)S(1)}, u32[]{:S(2)}, u32[]{:S(2)}) %collective-permute-start) | collective-permute-done | bytes 524320 | tf_op jit(solution)/shard_map/ppermute | solution.py:587
  17.3 7.4 %shard_map.67 = (bf16[32,64,128]{2,1,0:T(8,128)(2,1)}, f32[8,128]{1,0:T(8,128)}) custom-call(s32[1]{0:T(128)S(6)} %copy.9.where_ref, s32[8192,128]{1,0:T(8,128)} %bitcast.9, bf16[2048,128]{1,0:T(8,128)(2,1)S(1)} %collective-permute-done.recv_ref, f32[256,128]{1,0:T(8,128)} %get-tuple-element.11.taps_ref, bf16[1024,2048]{1,0:T(8,128)(2,1)} %get-tuple-element.12.table_hbm), custom_call_target="tpu_custom_call" | custom-call | tf_op jit(solution)/shard_map/pallas_call | solution.py:391
  24.7 6.1 %all-to-all-start = ((bf16[32,64,128]{2,1,0:T(8,128)(2,1)}), bf16[32,64,128]{2,1,0:T(8,128)(2,1)S(1)}, u32[]{:S(2)}, u32[]{:S(2)}) async-start(bf16[32,64,128]{2,1,0:T(8,128)(2,1)} %get-tuple-element.13), calls=%async_computation | async-start | bytes 1048576 | tf_op jit(solution)/shard_map/all_to_all | solution.py:592
  30.8 1.8 %collective-permute-start.1 = (bf16[2048,128]{1,0:T(8,128)(2,1)S(1)}, bf16[2048,128]{1,0:T(8,128)(2,1)S(1)}, u32[]{:S(2)}, u32[]{:S(2)}) collective-permute-start(bf16[2048,128]{1,0:T(8,128)(2,1)S(1)} %get-tuple-element.19), channel_id=1, source_target_pairs={{0,1},{1,0},{2,3},{3,2},{4,5},{5,4},{6,7},{7,6},{8,9},{9,8},{10,11... | collective-permute-start | bytes 1572872 | tf_op jit(solution)/shard_map/ppermute | solution.py:587
  32.7 17.8 %collective-permute-done.1.recv_ref = bf16[2048,128]{1,0:T(8,128)(2,1)S(1)} collective-permute-done((bf16[2048,128]{1,0:T(8,128)(2,1)S(1)}, bf16[2048,128]{1,0:T(8,128)(2,1)S(1)}, u32[]{:S(2)}, u32[]{:S(2)}) %collective-permute-start.1) | collective-permute-done | bytes 524320 | tf_op jit(solution)/shard_map/ppermute | solution.py:587
  50.5 0.0 copy-start.1
  50.5 7.8 %shard_map.68 = bf16[32,72,128]{2,1,0:T(8,128)(2,1)} custom-call(s32[1]{0:T(128)S(6)} %copy.9.where_ref, s32[8192,128]{1,0:T(8,128)} %bitcast.10, bf16[2048,128]{1,0:T(8,128)(2,1)S(1)} %collective-permute-done.1.recv_ref, f32[256,128]{1,0:T(8,128)} %get-tuple-element.11.taps_ref, bf16[1024,2048]{1,0:T(8,128)(2,1)} %get-tuple-element.12.table_hbm, ...), custom_call_target="tpu_custom_call" | custom-call | tf_op jit(solution)/shard_map/pallas_call | solution.py:391
  58.3 0.0 all-to-all-done.one_ref
  58.3 4.7 %all-to-all-start.1 = ((bf16[32,72,128]{2,1,0:T(8,128)(2,1)}), bf16[32,72,128]{2,1,0:T(8,128)(2,1)S(1)}, u32[]{:S(2)}, u32[]{:S(2)}) async-start(bf16[32,72,128]{2,1,0:T(8,128)(2,1)} %shard_map.68), calls=%async_computation.1 | async-start | bytes 1179648 | tf_op jit(solution)/shard_map/all_to_all | solution.py:594
  63.0 0.0 copy-done.1
  63.0 0.7 copy.8.picks_ref
  63.7 15.7 %all-to-all-done.1.two_ref = bf16[32,72,128]{2,1,0:T(8,128)(2,1)S(1)} async-done(((bf16[32,72,128]{2,1,0:T(8,128)(2,1)}), bf16[32,72,128]{2,1,0:T(8,128)(2,1)S(1)}, u32[]{:S(2)}, u32[]{:S(2)}) %all-to-all-start.1) | async-done | bytes 589856 | tf_op jit(solution)/shard_map/all_to_all | solution.py:594
  79.3 4.2 %subspace.1 = (bf16[8,512,128]{2,1,0:T(8,128)(2,1)S(1)}, f32[16,128]{1,0:T(8,128)}, f32[16,16]{1,0:T(8,128)}, f32[16,16]{1,0:T(8,128)}) custom-call(bf16[32,64,128]{2,1,0:T(8,128)(2,1)S(1)} %all-to-all-done.one_ref, bf16[32,72,128]{2,1,0:T(8,128)(2,1)S(1)} %all-to-all-done.1.two_ref, s32[8,1]{1,0:T(8,128)} %copy.8.picks_ref), custom_call_target="tpu_custom_call" | custom-call | tf_op jit(solution)/shard_map/subspace/pallas_call | solution.py:522
  83.6 1.8 %collective-permute-start.2 = (f32[16,16]{1,0:T(8,128)}, f32[16,16]{1,0:T(8,128)S(1)}, u32[]{:S(2)}, u32[]{:S(2)}) collective-permute-start(f32[16,16]{1,0:T(8,128)} %get-tuple-element.18), channel_id=1, source_target_pairs={{0,1},{1,0},{2,3},{3,2},{4,5},{5,4},{6,7},{7,6},{8,9},{9,8},{10,11... | collective-permute-start | bytes 3080 | tf_op jit(solution)/shard_map/ppermute | solution.py:596
  85.4 0.0 copy-start
  85.4 9.0 %covariance.1 = bf16[16,512,1024]{2,1,0:T(8,128)(2,1)} custom-call(bf16[8,512,128]{2,1,0:T(8,128)(2,1)S(1)} %get-tuple-element.15.x_ref), custom_call_target="tpu_custom_call" | custom-call | tf_op jit(solution)/shard_map/covariance/pallas_call | solution.py:564
  94.4 0.0 collective-permute-done.2
  94.4 0.0 copy-done
  94.4 0.7 fusion
Async XLA Ops:
  2.3 15.0 %collective-permute-start = (bf16[2048,128]{1,0:T(8,128)(2,1)S(1)}, bf16[2048,128]{1,0:T(8,128)(2,1)S(1)}, u32[]{:S(2)}, u32[]{:S(2)}) collective-permute-start(bf16[2048,128]{1,0:T(8,128)(2,1)S(1)} %get-tuple-element.20), channel_id=1, source_target_pairs={{0,1},{1,0},{2,3},{3,2},{4,5},{5,4},{6,7},{7,6},{8,9},{9,8},{10,11... | collective-permute-start | bytes 1572872 | tf_op jit(solution)/shard_map/ppermute | solution.py:587
  24.7 33.6 %all-to-all-start = ((bf16[32,64,128]{2,1,0:T(8,128)(2,1)}), bf16[32,64,128]{2,1,0:T(8,128)(2,1)S(1)}, u32[]{:S(2)}, u32[]{:S(2)}) async-start(bf16[32,64,128]{2,1,0:T(8,128)(2,1)} %get-tuple-element.13), calls=%async_computation | async-start | bytes 1048576 | tf_op jit(solution)/shard_map/all_to_all | solution.py:592
  30.8 19.7 %collective-permute-start.1 = (bf16[2048,128]{1,0:T(8,128)(2,1)S(1)}, bf16[2048,128]{1,0:T(8,128)(2,1)S(1)}, u32[]{:S(2)}, u32[]{:S(2)}) collective-permute-start(bf16[2048,128]{1,0:T(8,128)(2,1)S(1)} %get-tuple-element.19), channel_id=1, source_target_pairs={{0,1},{1,0},{2,3},{3,2},{4,5},{5,4},{6,7},{7,6},{8,9},{9,8},{10,11... | collective-permute-start | bytes 1572872 | tf_op jit(solution)/shard_map/ppermute | solution.py:587
  50.5 12.4 %copy-start.1 = (s32[8]{0:T(128)S(1)}, s32[8]{0:T(128)}, u32[]{:S(2)}) copy-start(s32[8]{0:T(128)} %param.7) | copy-start | bytes 100
  58.3 21.0 %all-to-all-start.1 = ((bf16[32,72,128]{2,1,0:T(8,128)(2,1)}), bf16[32,72,128]{2,1,0:T(8,128)(2,1)S(1)}, u32[]{:S(2)}, u32[]{:S(2)}) async-start(bf16[32,72,128]{2,1,0:T(8,128)(2,1)} %shard_map.68), calls=%async_computation.1 | async-start | bytes 1179648 | tf_op jit(solution)/shard_map/all_to_all | solution.py:594
  83.6 10.8 %collective-permute-start.2 = (f32[16,16]{1,0:T(8,128)}, f32[16,16]{1,0:T(8,128)S(1)}, u32[]{:S(2)}, u32[]{:S(2)}) collective-permute-start(f32[16,16]{1,0:T(8,128)} %get-tuple-element.18), channel_id=1, source_target_pairs={{0,1},{1,0},{2,3},{3,2},{4,5},{5,4},{6,7},{7,6},{8,9},{9,8},{10,11... | collective-permute-start | bytes 3080 | tf_op jit(solution)/shard_map/ppermute | solution.py:596
  85.4 9.0 %copy-start = (f32[16,16]{1,0:T(8,128)S(1)}, f32[16,16]{1,0:T(8,128)}, u32[]{:S(2)}) copy-start(f32[16,16]{1,0:T(8,128)} %get-tuple-element.17) | copy-start | bytes 3076
